TPU v7x, 32 devices: a whole 2x2x4 slice. The times are simulated.
32 devices in a mesh: shell: 8 (over z, core), patch: 4 (over y, x).
Axes of the slice: x: 2, y: 2, z: 4, core: 2. Of those that a mesh axis runs over, the one named last changes fastest.
Arguments:
- field_j: float32 [2, 256, 128, 128], P(None, 'shell', 'patch'), may hold values from -1 to 1
Outputs:
- beta_field: float32 [256, 128, 128], P('shell', 'patch')
- u_field: float32 [2, 256, 128, 128], P(None, 'shell', 'patch')
- w_field: float32 [256, 128, 128], P('shell', 'patch')
- h_field: float32 [2, 256, 128, 128], P(None, 'shell', 'patch')
All inputs are finite; a program needn't handle non-finite values.
Results may differ from a plain program's by a relative error of at most 0.00002.
Values sent between devices are 32-bit elements; how exact they have to be, the bound alone decides.
A program may use at most 64 MiB of HBM per device.

v0:
```python
import functools
import math

import jax
import jax.numpy as jnp
from jax import lax
from jax.experimental import pallas as pl
from jax.experimental.pallas import tpu as pltpu
from jax.sharding import PartitionSpec as P

PAD = 8


def remote(src, dst, send_sem, recv_sem, shell, patch):
    return pltpu.make_async_remote_copy(
        src_ref=src,
        dst_ref=dst,
        send_sem=send_sem,
        recv_sem=recv_sem,
        device_id=(shell, patch),
        device_id_type=pl.DeviceIdType.MESH,
    )


def kernel(shells, patches, step, j_hbm, bp, up, cw, ch, below_h,
           jp, jnext, jedge, jhalo, barj, bedge, bhalo, uedge, uhalo, gs,
           below_b, sum_b, part_b, tot_b, slot_b, pre_b,
           below_u, sum_u, part_u, tot_u, slot_u, pre_u,
           sum_h, part_h, tot_h, slot_h, pre_h,
           rim_b, rtot_b, rpart_b, rslot_b, rim_u, rtot_u, rpart_u, rslot_u,
           load_sem, rad_sem, edge_send, edge_recv, part_sem, send_sem, recv_sem, fwd_sem,
           rpart_send, rpart_recv, rim_send, rim_recv):
    radii, cols, lanes = jp.shape[1], jp.shape[2] - 2 * PAD, jp.shape[3]
    chips = shells // 2
    shell, patch = lax.axis_index("shell"), lax.axis_index("patch")
    chip, core = shell // 2, shell % 2
    partner = shell + 1 - 2 * core
    right = lax.rem(patch + 1, patches)
    left = lax.rem(patch + patches - 1, patches)
    inner = slice(PAD, PAD + cols)
    above = slice(PAD + 1, PAD + cols + 1)
    below = slice(PAD - 1, PAD + cols - 1)
    before, after = slice(PAD - 1, PAD), slice(PAD + cols, PAD + cols + 1)

    load = pltpu.make_async_copy(j_hbm, jp.at[:, :, pl.ds(PAD, cols), :], load_sem)
    load.start()
    barrier = pltpu.get_barrier_semaphore()
    for d in range(shells):
        there = lax.rem(shell + d, shells)
        for p in (patch, left, right):
            if d == 0 and p is patch:
                continue
            pl.semaphore_signal(barrier, inc=1, device_id=(there, p),
                                device_id_type=pl.DeviceIdType.MESH)

    lane = lax.broadcasted_iota(jnp.int32, (8, lanes), 1)
    keep_f = jnp.where(lane == lanes - 1, 0.0, 0.5).astype(jnp.float32)
    keep_b = jnp.where(lane == 0, 0.0, 0.5).astype(jnp.float32)

    def theta(x):
        reps = x.shape[0] // 8
        mf = jnp.concatenate([keep_f] * reps, axis=0) if reps > 1 else keep_f
        mb = jnp.concatenate([keep_b] * reps, axis=0) if reps > 1 else keep_b
        return pltpu.roll(x, lanes - 1, 1) * mf - pltpu.roll(x, 1, 1) * mb

    def halo(edge, got, field):
        to_left = remote(edge.at[0], got.at[1], edge_send.at[field, 0], edge_recv.at[field, 1], shell, left)
        to_right = remote(edge.at[1], got.at[0], edge_send.at[field, 1], edge_recv.at[field, 0], shell, right)
        return to_left, to_right

    def pieces(stage, own, part, tot, slots, both):
        half = own.shape[0] // 2
        mine = pl.ds(pl.multiple_of(core * half, 8), half)
        first = remote(own, part, part_sem.at[stage, 0], part_sem.at[stage, 1], partner, patch)
        sends = []
        for d in range(1, chips):
            if both:
                sends.append([
                    remote(tot.at[mine], slots.at[d - 1, mine], send_sem.at[stage, d - 1, e],
                           recv_sem.at[stage, d - 1, core], (chip + d) * 2 + e, patch)
                    for e in range(2)])
            else:
                sends.append([
                    remote(tot.at[mine], slots.at[d - 1, mine], send_sem.at[stage, d - 1, 0],
                           recv_sem.at[stage, d - 1, 0], (chip + d) * 2 + core, patch)])
        return mine, half, first, sends

    def rim_pieces(stage, rim, rtot, rpart, rslot):
        over = left * (1 - core) + right * core
        near = [
            remote(rim.at[0], rpart.at[1], rpart_send.at[stage, 0], rpart_recv.at[stage, 1], partner, left),
            remote(rim.at[1], rpart.at[0], rpart_send.at[stage, 1], rpart_recv.at[stage, 0], partner, right)]
        far = [[
            remote(rtot.at[core], rslot.at[d - 1, 1 - core], rim_send.at[stage, d - 1, e],
                   rim_recv.at[stage, d - 1, 1 - core], (chip + d) * 2 + e, over)
            for e in range(2)] for d in range(1, chips)]
        return near, far

    def exchange(stage, own, part, tot, slots, pre, out, both, rims=None):
        mine, half, first, sends = pieces(stage, own, part, tot, slots, both)
        first.start()
        if rims is not None:
            rim, rtot, rpart, rslot = rims
            fields = rim.shape[1]
            cols_of = own.shape[0] // fields
            for f in range(fields):
                rim[0, f:f + 1] = own[f * cols_of:f * cols_of + 1]
                rim[1, f:f + 1] = own[(f + 1) * cols_of - 1:(f + 1) * cols_of]
            near, far = rim_pieces(stage, rim, rtot, rpart, rslot)

            @pl.when(core == 0)
            def _():
                for copy in near:
                    copy.start()

        first.wait_recv()
        tot[mine] = own[mine] + part[mine]
        if rims is not None:
            for f in range(fields):
                lo, hi = f * cols_of, (f + 1) * cols_of - 1
                rtot[0, f:f + 1] = own[lo:lo + 1] + part[lo:lo + 1]
                rtot[1, f:f + 1] = own[hi:hi + 1] + part[hi:hi + 1]
        for d in range(1, chips):
            @pl.when(chip + d < chips)
            def _():
                for copy in sends[d - 1]:
                    copy.start()
                if rims is not None:
                    for copy in far[d - 1]:
                        copy.start()

        @pl.when(core == 0)
        def _():
            out[...] = jnp.zeros_like(out)

        @pl.when(core == 1)
        def _():
            out[...] = part[...]
            if rims is not None:
                for copy in near:
                    copy.wait_recv()

        if rims is not None:
            @pl.when(core == 0)
            def _():
                rpart[...] = jnp.zeros_like(rpart)

        if both:
            for d in range(1, chips):
                @pl.when(chip >= d)
                def _():
                    for e in range(2):
                        piece = pl.ds(e * half, half)
                        remote(tot.at[piece], slots.at[d - 1, piece], send_sem.at[stage, d - 1, e],
                               recv_sem.at[stage, d - 1, e], shell, patch).wait_recv()
                    out[...] += slots[d - 1]
        else:
            @pl.when(chip > 0)
            def _():
                pre[mine] = jnp.zeros((half, lanes), jnp.float32)

            for d in range(1, chips):
                @pl.when(chip >= d)
                def _():
                    for copy in sends[d - 1]:
                        copy.wait_recv()
                    pre[mine] += slots[d - 1, mine]

            @pl.when(chip > 0)
            def _():
                fwd = remote(pre.at[mine], pre.at[mine], fwd_sem.at[stage, 0], fwd_sem.at[stage, 1],
                             partner, patch)
                fwd.start()
                fwd.wait_recv()
                out[...] += pre[...]

        if rims is not None:
            for d in range(1, chips):
                @pl.when(chip >= d)
                def _():
                    for e in range(2):
                        remote(rtot.at[e], rslot.at[d - 1, e], rim_send.at[stage, d - 1, 0],
                               rim_recv.at[stage, d - 1, e], shell, patch).wait_recv()
                    rpart[...] += rslot[d - 1]

    def finish(stage, own, part, tot, slots, pre, both, rims=None):
        mine, half, first, sends = pieces(stage, own, part, tot, slots, both)
        first.wait_send()
        if rims is not None:
            near, far = rim_pieces(stage, *rims)

            @pl.when(core == 0)
            def _():
                for copy in near:
                    copy.wait_send()

        for d in range(1, chips):
            @pl.when(chip + d < chips)
            def _():
                for copy in sends[d - 1]:
                    copy.wait_send()
                if rims is not None:
                    for copy in far[d - 1]:
                        copy.wait_send()

        if not both:
            @pl.when(chip > 0)
            def _():
                remote(pre.at[mine], pre.at[mine], fwd_sem.at[stage, 0], fwd_sem.at[stage, 1],
                       partner, patch).wait_send()

    load.wait()

    def pack(k, c):
        for f in range(2):
            jedge[0, f, pl.ds(k, 1), :] = jp[f, k, PAD:PAD + 1, :]
            jedge[1, f, pl.ds(k, 1), :] = jp[f, k, PAD + cols - 1:PAD + cols, :]
        return c

    lax.fori_loop(0, radii, pack, 0, unroll=8)
    pl.semaphore_wait(barrier, 3 * shells - 1)

    j_left, j_right = halo(jedge, jhalo, 0)
    j_left.start()
    j_right.start()

    @pl.when(shell > 0)
    def _():
        remote(j_hbm.at[:, 0], jnext, rad_sem.at[0], rad_sem.at[1], shell - 1, patch).start()

    def beta_step(k, next_of, spans, totals):
        new = []
        for (lo, n), total in zip(spans, totals):
            at = slice(PAD + lo, PAD + lo + n)
            up1 = slice(PAD + lo + 1, PAD + lo + n + 1)
            dn1 = slice(PAD + lo - 1, PAD + lo + n - 1)
            a, b = jp[0, k, at], jp[1, k, at]
            ra, rb = next_of(0, k, lo, n) - a, next_of(1, k, lo, n) - b
            ta, tb = theta(a), theta(b)
            pa = 0.5 * (jp[0, k, up1] - jp[0, k, dn1])
            pb = 0.5 * (jp[1, k, up1] - jp[1, k, dn1])
            ea, eb = ta - pb, tb + pa
            barj[0, k, lo:lo + n] = ta + pb
            barj[1, k, lo:lo + n] = tb - pa
            total = total + 0.25 * (0.5 * (ra * ra + rb * rb) - (ea * ea + eb * eb))
            bp[k, at] = total
            if lo == 0:
                bedge[0, pl.ds(k, 1), :] = total[:1]
            if lo + n == cols:
                bedge[1, pl.ds(k, 1), :] = total[n - 1:]
            new.append(total)
        return tuple(new)

    def from_jp(f, k, lo, n):
        return jp[f, k + 1, PAD + lo:PAD + lo + n]

    def from_next(f, k, lo, n):
        return jnext[f, lo:lo + n]

    def beta_span(spans, middle):
        zeros = tuple(jnp.zeros((n, lanes), jnp.float32) for _, n in spans)
        totals = lax.fori_loop(0, radii - 1, lambda k, t: beta_step(k, from_jp, spans, t), zeros, unroll=2)
        middle()
        totals = beta_step(radii - 1, from_next, spans, totals)
        for (lo, n), total in zip(spans, totals):
            sum_b[lo:lo + n] = total

    def wait_next():
        @pl.when(shell == shells - 1)
        def _():
            for f in range(2):
                jnext[f] = jp[f, radii - 1, inner]

        @pl.when(shell < shells - 1)
        def _():
            remote(j_hbm.at[:, 0], jnext, rad_sem.at[0], rad_sem.at[1], shell, patch).wait_recv()

    beta_span(((8, cols - 16),), wait_next)
    j_left.wait_recv()
    j_right.wait_recv()

    def unpack(k, c):
        for f in range(2):
            jp[f, k, before, :] = jhalo[0, f, pl.ds(k, 1), :]
            jp[f, k, after, :] = jhalo[1, f, pl.ds(k, 1), :]
        return c

    lax.fori_loop(0, radii, unpack, 0, unroll=8)
    beta_span(((0, 8), (cols - 8, 8)), lambda: None)

    b_left, b_right = halo(bedge, bhalo, 1)
    b_left.start()
    b_right.start()
    rims_b = (rim_b, rtot_b, rpart_b, rslot_b)
    exchange(0, sum_b, part_b, tot_b, slot_b, pre_b, below_b, True, rims_b)
    b_left.wait_recv()
    b_right.wait_recv()

    def beta_final(k, c):
        bp[k, inner] = step * (bp[k, inner] + below_b[...])
        bp[k, before] = step * (bhalo[0, pl.ds(k, 1), :] + rpart_b[0])
        bp[k, after] = step * (bhalo[1, pl.ds(k, 1), :] + rpart_b[1])
        return c

    lax.fori_loop(0, radii, beta_final, 0, unroll=2)
    zero = jnp.zeros((cols, lanes), jnp.float32)

    def u_step(k, carry):
        sa, sb = carry
        beta = bp[k, inner]
        growth = jnp.exp(2.0 * beta)
        gs[k] = growth
        br = theta(beta)
        bi = 0.5 * (bp[k, above] - bp[k, below])
        a, b = jp[0, k, inner], jp[1, k, inner]
        sa = sa + growth * (br - (a * br + b * bi))
        sb = sb + growth * (bi - (b * br - a * bi))
        for f, s in ((0, sa), (1, sb)):
            up[f, k, inner] = s
            uedge[0, f, pl.ds(k, 1), :] = s[:1]
            uedge[1, f, pl.ds(k, 1), :] = s[cols - 1:]
        return sa, sb

    sa, sb = lax.fori_loop(0, radii, u_step, (zero, zero), unroll=2)
    sum_u[:cols] = sa
    sum_u[cols:] = sb
    u_left, u_right = halo(uedge, uhalo, 2)
    u_left.start()
    u_right.start()
    rims_u = (rim_u, rtot_u, rpart_u, rslot_u)
    exchange(1, sum_u, part_u, tot_u, slot_u, pre_u, below_u, False, rims_u)
    u_left.wait_recv()
    u_right.wait_recv()

    def u_final(k, c):
        for f in range(2):
            up[f, k, inner] = step * (up[f, k, inner] + below_u[f * cols:(f + 1) * cols])
            up[f, k, before] = step * (uhalo[0, f, pl.ds(k, 1), :] + rpart_u[0, f:f + 1])
            up[f, k, after] = step * (uhalo[1, f, pl.ds(k, 1), :] + rpart_u[1, f:f + 1])
        return c

    lax.fori_loop(0, radii, u_final, 0, unroll=2)

    def wh_step(k, carry):
        sw, sa, sb = carry
        beta = bp[k, inner]
        growth = gs[k]
        a, b = jp[0, k, inner], jp[1, k, inner]
        ua, ub = up[0, k, inner], up[1, k, inner]
        ta, tb = theta(ua), theta(ub)
        pa = 0.5 * (up[0, k, above] - up[0, k, below])
        pb = 0.5 * (up[1, k, above] - up[1, k, below])
        ja, jb = barj[0, k], barj[1, k]
        sw = sw + (growth * (ta + pb) + (b * ua - a * ub))
        sa = sa + ((ta - pb) + ua * ja - ub * jb + beta * a)
        sb = sb + ((tb + pa) + ua * jb + ub * ja + beta * b)
        cw[k] = sw
        ch[0, k] = sa
        ch[1, k] = sb
        return sw, sa, sb

    sw, sa, sb = lax.fori_loop(0, radii, wh_step, (zero, zero, zero))
    sum_h[:cols] = sw
    sum_h[cols:2 * cols] = sa
    sum_h[2 * cols:] = sb
    exchange(2, sum_h, part_h, tot_h, slot_h, pre_h, below_h, False)

    for copy in (j_left, j_right, b_left, b_right, u_left, u_right):
        copy.wait_send()

    @pl.when(shell > 0)
    def _():
        remote(j_hbm.at[:, 0], jnext, rad_sem.at[0], rad_sem.at[1], shell - 1, patch).wait_send()

    finish(0, sum_b, part_b, tot_b, slot_b, pre_b, True, rims_b)
    finish(1, sum_u, part_u, tot_u, slot_u, pre_u, False, rims_u)
    finish(2, sum_h, part_h, tot_h, slot_h, pre_h, False)


def tail(step, bp, up, cw, ch, below_h, beta_out, u_out, w_out, h_out, wv, hv, sems):
    radii, cols = cw.shape[0], cw.shape[1]
    rows = pl.ds(PAD, cols)
    copies = [pltpu.make_async_copy(bp.at[:, rows, :], beta_out, sems.at[0, 0])]
    copies += [pltpu.make_async_copy(up.at[f, :, rows, :], u_out.at[f], sems.at[1, f]) for f in range(2)]
    for copy in copies:
        copy.start()
    parts = 2
    size = radii // parts
    for i in range(parts):
        def wh_final(k, c):
            wv[k] = step * (cw[k] + below_h[:cols])
            for f in range(2):
                hv[f, k] = step * (ch[f, k] + below_h[(f + 1) * cols:(f + 2) * cols])
            return c

        lax.fori_loop(i * size, (i + 1) * size, wh_final, 0, unroll=4)
        at = pl.ds(i * size, size)
        more = [pltpu.make_async_copy(wv.at[at], w_out.at[at], sems.at[2, i]),
                pltpu.make_async_copy(hv.at[:, at], h_out.at[:, at], sems.at[3, i])]
        for copy in more:
            copy.start()
        copies += more
    for copy in copies:
        copy.wait()


def solution(mesh):
    shells, patches = mesh.shape["shell"], mesh.shape["patch"]
    chips = shells // 2

    def local(field_j):
        _, radii, cols, lanes = field_j.shape
        step = 1.0 / math.sqrt(radii * shells)
        f32 = jnp.float32
        vm = lambda *s: pltpu.VMEM(s, f32)
        tall = cols + 2 * PAD
        scratch = [
            vm(2, radii, tall, lanes), vm(2, cols, lanes), vm(2, 2, radii, lanes), vm(2, 2, radii, lanes),
            vm(2, radii, cols, lanes),
            vm(2, radii, lanes), vm(2, radii, lanes),
            vm(2, 2, radii, lanes), vm(2, 2, radii, lanes), vm(radii, cols, lanes),
        ]
        many = max(chips - 1, 1)
        for n in (1, 2, 3):
            if n < 3:
                scratch.append(vm(n * cols, lanes))
            scratch += [vm(n * cols, lanes)] * 3 + [vm(many, n * cols, lanes), vm(n * cols, lanes)]
        for n in (1, 2):
            scratch += [vm(2, n, lanes)] * 3 + [vm(many, 2, n, lanes)]
        dma = pltpu.SemaphoreType.DMA
        scratch += [dma, dma((2,)), dma((3, 2)), dma((3, 2)), dma((3, 2)),
                    dma((3, many, 2)), dma((3, many, 2)), dma((3, 2)),
                    dma((2, 2)), dma((2, 2)), dma((2, many, 2)), dma((2, many, 2))]
        shape = lambda *s: jax.ShapeDtypeStruct(s, f32)
        vmem = pl.BlockSpec(memory_space=pltpu.VMEM)
        hbm = pl.BlockSpec(memory_space=pltpu.HBM)
        found = pl.pallas_call(
            functools.partial(kernel, shells, patches, step),
            out_shape=(shape(radii, tall, lanes), shape(2, radii, tall, lanes), shape(radii, cols, lanes),
                       shape(2, radii, cols, lanes), shape(3 * cols, lanes)),
            in_specs=[hbm],
            out_specs=(vmem,) * 5,
            scratch_shapes=scratch,
            compiler_params=pltpu.CompilerParams(
                collective_id=0, has_side_effects=True, vmem_limit_bytes=24 * 1024 * 1024),
        )(pltpu.with_memory_space_constraint(field_j, pltpu.HBM))
        return pl.pallas_call(
            functools.partial(tail, step),
            out_shape=(shape(radii, cols, lanes), shape(2, radii, cols, lanes), shape(radii, cols, lanes),
                       shape(2, radii, cols, lanes)),
            in_specs=[vmem] * 5,
            out_specs=(hbm,) * 4,
            scratch_shapes=[vm(radii, cols, lanes), vm(2, radii, cols, lanes), dma((4, 2))],
            compiler_params=pltpu.CompilerParams(vmem_limit_bytes=24 * 1024 * 1024),
        )(*found)

    return jax.shard_map(
        local,
        mesh=mesh,
        in_specs=(P(None, "shell", "patch", None),),
        out_specs=(
            P("shell", "patch", None),
            P(None, "shell", "patch", None),
            P("shell", "patch", None),
            P(None, "shell", "patch", None),
        ),
        check_vma=False,
    )
```

profile of v0, /device:TPU:25, one launch (start us, length us, event | category | flops | bytes accessed | tf_op | source)
XLA Modules:
  0.0 32.0 jit_solution(6186015774632515795)
XLA Ops:
  0.6 29.6 %shard_map.46 = (f32[32,48,128]{2,1,0:T(8,128)S(1)}, f32[2,32,48,128]{3,2,1,0:T(8,128)S(1)}, f32[32,32,128]{2,1,0:T(8,128)S(1)}, f32[2,32,32,128]{3,2,1,0:T(8,128)S(1)}, f32[96,128]{1,0:T(8,128)S(1)}) custom-call(f32[2,32,32,128]{3,2,1,0:T(8,128)} %j_hbm.1), custom_call_target="tpu_custom_call" | custom-call | tf_op jit(solution)/shard_map/pallas_call | solution.py:437
  30.2 1.7 %shard_map.47 = (f32[32,32,128]{2,1,0:T(8,128)}, f32[2,32,32,128]{3,2,1,0:T(8,128)}, f32[32,32,128]{2,1,0:T(8,128)}, f32[2,32,32,128]{3,2,1,0:T(8,128)}) custom-call(f32[32,48,128]{2,1,0:T(8,128)S(1)} %get-tuple-element.9.bp, f32[2,32,48,128]{3,2,1,0:T(8,128)S(1)} %get-tuple-element.10.up, f32[32,32,128]{2,1,0:T(8,128)S(1)} %get-tuple-element.11.cw, ...), custom_call_target="tpu_custom_call" | custom-call | tf_op jit(solution)/shard_map/pallas_call | solution.py:447
where the time goes:
time: 32.1 us; the launch traced here: 32 us
  Pallas kernels  31.3 us (98%)
  between operations  0.64 us (2%)
    pallas_call x1, Pallas kernels, local(): pl.pallas_call(functools.partial(kernel, shells, patches, step), out_shap...  29.6 us
    pallas_call x1, Pallas kernels, local(): pl.pallas_call(functools.partial(tail, step), out_shape=(shape(radii, col...  1.73 us

commit v1 on v0

v1 whole, which is shorter than its diff:
```python
import functools
import math

import jax
import jax.numpy as jnp
from jax import lax
from jax.experimental import pallas as pl
from jax.experimental.pallas import tpu as pltpu
from jax.sharding import PartitionSpec as P

PAD = 8
LAP = 4


def remote(src, dst, send_sem, recv_sem, shell, patch):
    return pltpu.make_async_remote_copy(
        src_ref=src,
        dst_ref=dst,
        send_sem=send_sem,
        recv_sem=recv_sem,
        device_id=(shell, patch),
        device_id_type=pl.DeviceIdType.MESH,
    )


def make_theta(lanes):
    lane = lax.broadcasted_iota(jnp.int32, (8, lanes), 1)
    keep_f = jnp.where(lane == lanes - 1, 0.0, 0.5).astype(jnp.float32)
    keep_b = jnp.where(lane == 0, 0.0, 0.5).astype(jnp.float32)

    def theta(x):
        reps = x.shape[0] // 8
        mf = jnp.concatenate([keep_f] * reps, axis=0) if reps > 1 else keep_f
        mb = jnp.concatenate([keep_b] * reps, axis=0) if reps > 1 else keep_b
        return pltpu.roll(x, lanes - 1, 1) * mf - pltpu.roll(x, 1, 1) * mb

    return theta


def kernel(shells, patches, step, j_hbm, jp, up, bfin, gs, barj, cw, ch, pre,
           bp, es, dr, jnext, jedge, jhalo, bedge, bhalo,
           sum_b, slot_b, slot_l, slot_r, bt, su, seg_e, seg_l, slot_e, slot_s, acc, fsrc, fslot,
           load_sem, rad_sem, jh_send, jh_recv, bh_send, bh_recv,
           b_send, b_recv, e_send, e_recv, s_send, s_recv, f_sem):
    radii, cols, lanes = jp.shape[1], jp.shape[2] - 2 * PAD, jp.shape[3]
    chips = shells // 2
    half = cols // 2
    wide = half + 2 * LAP
    tall = cols + 8
    f32 = jnp.float32
    shell, patch = lax.axis_index("shell"), lax.axis_index("patch")
    chip, core = shell // 2, shell % 2
    partner = shell + 1 - 2 * core
    right = lax.rem(patch + 1, patches)
    left = lax.rem(patch + patches - 1, patches)
    inner = slice(PAD, PAD + cols)
    above = slice(PAD + 1, PAD + cols + 1)
    below = slice(PAD - 1, PAD + cols - 1)
    before, after = slice(PAD - 1, PAD), slice(PAD + cols, PAD + cols + 1)
    theta = make_theta(lanes)

    load = pltpu.make_async_copy(j_hbm, jp.at[:, :, pl.ds(PAD, cols), :], load_sem)
    load.start()
    barrier = pltpu.get_barrier_semaphore()
    for d in range(shells):
        there = lax.rem(shell + d, shells)
        for p in (patch, left, right):
            if d == 0 and p is patch:
                continue
            pl.semaphore_signal(barrier, inc=1, device_id=(there, p),
                                device_id_type=pl.DeviceIdType.MESH)

    def halo(edge, got, send, recv):
        to_left = remote(edge.at[0], got.at[1], send.at[0], recv.at[1], shell, left)
        to_right = remote(edge.at[1], got.at[0], send.at[1], recv.at[0], shell, right)
        return to_left, to_right

    load.wait()

    def pack(k, c):
        for f in range(2):
            jedge[0, f, pl.ds(k, 1), :] = jp[f, k, PAD:PAD + 1, :]
            jedge[1, f, pl.ds(k, 1), :] = jp[f, k, PAD + cols - 1:PAD + cols, :]
        return c

    lax.fori_loop(0, radii, pack, 0, unroll=8)
    pl.semaphore_wait(barrier, 3 * shells - 1)

    j_left, j_right = halo(jedge, jhalo, jh_send, jh_recv)
    j_left.start()
    j_right.start()

    @pl.when(shell > 0)
    def _():
        remote(j_hbm.at[:, 0], jnext, rad_sem.at[0], rad_sem.at[1], shell - 1, patch).start()

    def beta_step(k, next_of, spans, totals):
        new = []
        for (lo, n), total in zip(spans, totals):
            at = slice(PAD + lo, PAD + lo + n)
            up1 = slice(PAD + lo + 1, PAD + lo + n + 1)
            dn1 = slice(PAD + lo - 1, PAD + lo + n - 1)
            a, b = jp[0, k, at], jp[1, k, at]
            ra, rb = next_of(0, k, lo, n) - a, next_of(1, k, lo, n) - b
            ta, tb = theta(a), theta(b)
            pa = 0.5 * (jp[0, k, up1] - jp[0, k, dn1])
            pb = 0.5 * (jp[1, k, up1] - jp[1, k, dn1])
            ea, eb = ta - pb, tb + pa
            barj[0, k, lo:lo + n] = ta + pb
            barj[1, k, lo:lo + n] = tb - pa
            total = total + 0.25 * (0.5 * (ra * ra + rb * rb) - (ea * ea + eb * eb))
            bp[k, at] = total
            if lo == 0:
                bedge[0, 0, pl.ds(k, 1), :] = total[:1]
                bedge[0, 1, pl.ds(k, 1), :] = total[1:2]
            if lo + n == cols:
                bedge[1, 0, pl.ds(k, 1), :] = total[n - 2:n - 1]
                bedge[1, 1, pl.ds(k, 1), :] = total[n - 1:]
            new.append(total)
        return tuple(new)

    def from_jp(f, k, lo, n):
        return jp[f, k + 1, PAD + lo:PAD + lo + n]

    def from_next(f, k, lo, n):
        return jnext[f, lo:lo + n]

    def beta_span(spans, middle):
        zeros = tuple(jnp.zeros((n, lanes), f32) for _, n in spans)
        totals = lax.fori_loop(0, radii - 1, lambda k, t: beta_step(k, from_jp, spans, t), zeros, unroll=2)
        middle()
        totals = beta_step(radii - 1, from_next, spans, totals)
        for (lo, n), total in zip(spans, totals):
            sum_b[lo:lo + n] = total

    def wait_next():
        @pl.when(shell == shells - 1)
        def _():
            for f in range(2):
                jnext[f] = jp[f, radii - 1, inner]

        @pl.when(shell < shells - 1)
        def _():
            remote(j_hbm.at[:, 0], jnext, rad_sem.at[0], rad_sem.at[1], shell, patch).wait_recv()

    beta_span(((8, cols - 16),), wait_next)
    j_left.wait_recv()
    j_right.wait_recv()

    def unpack(k, c):
        for f in range(2):
            jp[f, k, before, :] = jhalo[0, f, pl.ds(k, 1), :]
            jp[f, k, after, :] = jhalo[1, f, pl.ds(k, 1), :]
        return c

    lax.fori_loop(0, radii, unpack, 0, unroll=8)
    beta_span(((0, 8), (cols - 8, 8)), lambda: None)

    def b_copies(d):
        there = shell + d
        return [
            remote(sum_b, slot_b.at[d - 1], b_send.at[0, d - 1], b_recv.at[0, d - 1], there, patch),
            remote(sum_b.at[pl.ds(cols - 8, 8)], slot_l.at[d - 1], b_send.at[1, d - 1], b_recv.at[1, d - 1],
                   there, right),
            remote(sum_b.at[pl.ds(0, 8)], slot_r.at[d - 1], b_send.at[2, d - 1], b_recv.at[2, d - 1],
                   there, left),
        ]

    b_left, b_right = halo(bedge, bhalo, bh_send, bh_recv)
    for d in range(1, shells):
        @pl.when(shell + d < shells)
        def _():
            for copy in b_copies(d):
                copy.start()
        if d == 1:
            b_left.start()
            b_right.start()

    zero = jnp.zeros((cols, lanes), f32)

    def local_step(k, carry):
        se, sa, sb, sja, sjb, sba, sbb = carry
        beta = bp[k, inner]
        grow = jnp.exp((2.0 * step) * beta)
        es[k, inner] = grow
        dr[k, inner] = theta(beta)
        a, b = jp[0, k, inner], jp[1, k, inner]
        return (se + grow, sa + a, sb + b, sja + barj[0, k], sjb + barj[1, k], sba + beta * a, sbb + beta * b)

    se, sa, sb, sja, sjb, sba, sbb = lax.fori_loop(0, radii, local_step, (zero,) * 7, unroll=2)
    for c in range(2):
        rows = slice(c * half, (c + 1) * half)
        for i, x in enumerate((sa, sb, sja, sjb)):
            seg_e[c, i * half:(i + 1) * half] = x[rows]

    def seg_copies(dz, seg, slot, send, recv):
        return [remote(seg.at[e], slot.at[(dz - 1) * 2 + core], send.at[(dz - 1) * 2 + e],
                       recv.at[(dz - 1) * 2 + core], (chip + dz) * 2 + e, patch) for e in range(2)]

    def own_copy(seg, slot, send, recv):
        last = 2 * (chips - 1)
        return remote(seg.at[1], slot.at[last], send.at[last], recv.at[last], partner, patch)

    def start_seg(seg, slot, send, recv):
        @pl.when(core == 0)
        def _():
            own_copy(seg, slot, send, recv).start()

        for dz in range(chips - 1, 0, -1):
            @pl.when(chip + dz < chips)
            def _():
                for copy in seg_copies(dz, seg, slot, send, recv):
                    copy.start()

    start_seg(seg_e, slot_e, e_send, e_recv)

    b_left.wait_recv()
    b_right.wait_recv()

    def halo_step(k, c):
        bp[k, PAD - 2:PAD - 1, :] = bhalo[0, 0, pl.ds(k, 1), :]
        bp[k, PAD - 1:PAD, :] = bhalo[0, 1, pl.ds(k, 1), :]
        bp[k, PAD + cols:PAD + cols + 1, :] = bhalo[1, 0, pl.ds(k, 1), :]
        bp[k, PAD + cols + 1:PAD + cols + 2, :] = bhalo[1, 1, pl.ds(k, 1), :]
        return c

    lax.fori_loop(0, radii, halo_step, 0, unroll=8)

    def halo_exp(k, c):
        for lo in (0, PAD + cols):
            x = bp[k, lo:lo + 8]
            es[k, lo:lo + 8] = jnp.exp((2.0 * step) * x)
            dr[k, lo:lo + 8] = theta(x)
        return c

    lax.fori_loop(0, radii, halo_exp, 0, unroll=4)

    bt[...] = jnp.zeros_like(bt)
    for d in range(1, shells):
        @pl.when(shell >= d)
        def _():
            for i, slot in enumerate((slot_b, slot_l, slot_r)):
                src = (sum_b, sum_b.at[pl.ds(0, 8)], sum_b.at[pl.ds(0, 8)])[i]
                remote(src, slot.at[d - 1], b_send.at[i, d - 1], b_recv.at[i, d - 1], shell, patch).wait_recv()
            bt[inner] += slot_b[d - 1]
            bt[0:PAD] += slot_l[d - 1]
            bt[PAD + cols:] += slot_r[d - 1]

    first = PAD - 1
    mid, hi, lo = slice(first, first + tall), slice(first + 1, first + tall + 1), slice(first - 1, first + tall - 1)
    base_r = theta(bt[mid])
    base_i = bt[hi] - bt[lo]
    base_g = step * jnp.exp((2.0 * step) * bt[mid])
    wide_zero = jnp.zeros((tall, lanes), f32)

    def u_step(k, carry):
        sa, sb = carry
        growth = base_g * es[k, mid]
        br = dr[k, mid] + base_r
        bi = 0.5 * ((bp[k, hi] - bp[k, lo]) + base_i)
        a, b = jp[0, k, mid], jp[1, k, mid]
        sa = sa + growth * (br - (a * br + b * bi))
        sb = sb + growth * (bi - (b * br - a * bi))
        up[0, k, mid] = sa
        up[1, k, mid] = sb
        return sa, sb

    ua_sum, ub_sum = lax.fori_loop(0, radii, u_step, (wide_zero, wide_zero), unroll=2)
    su[0, mid] = ua_sum
    su[1, mid] = ub_sum

    def sums_step(k, carry):
        w1, w2, q, qa, ub_all, ha, hb = carry
        a, b = jp[0, k, inner], jp[1, k, inner]
        ua, ub = up[0, k, inner], up[1, k, inner]
        ta = theta(ua)
        pb = 0.5 * (up[1, k, above] - up[1, k, below])
        ja, jb = barj[0, k], barj[1, k]
        w1 = w1 + es[k, inner] * (ta + pb)
        w2 = w2 + (b * ua - a * ub)
        q = q + (ta - pb)
        qa = qa + (up[0, k, above] - up[0, k, below])
        ub_all = ub_all + ub
        ha = ha + (ua * ja - ub * jb)
        hb = hb + (ua * jb + ub * ja)
        return w1, w2, q, qa, ub_all, ha, hb

    w1, w2, q, qa, ub_all, ha, hb = lax.fori_loop(0, radii, sums_step, (zero,) * 7, unroll=2)
    full_b = bt[inner]
    grow_b = jnp.exp((2.0 * step) * full_b)
    planes = (grow_b * se, grow_b * w1 + w2, q + ha + (sba + full_b * sa),
              theta(ub_all) + 0.5 * qa + hb + (sbb + full_b * sb))
    for c in range(2):
        for f in range(2):
            start = PAD + c * half - LAP
            seg_l[c, f * wide:(f + 1) * wide] = su[f, start:start + wide]
        for i, x in enumerate(planes):
            at = 2 * wide + i * half
            seg_l[c, at:at + half] = x[c * half:(c + 1) * half]

    start_seg(seg_l, slot_s, s_send, s_recv)

    def wh_step(k, carry):
        sw, sa, sb = carry
        beta = bp[k, inner] + full_b
        bfin[k] = step * beta
        growth = grow_b * es[k, inner]
        gs[k] = growth
        a, b = jp[0, k, inner], jp[1, k, inner]
        ua, ub = up[0, k, inner], up[1, k, inner]
        ta, tb = theta(ua), theta(ub)
        pa = 0.5 * (up[0, k, above] - up[0, k, below])
        pb = 0.5 * (up[1, k, above] - up[1, k, below])
        ja, jb = barj[0, k], barj[1, k]
        sw = sw + (growth * (ta + pb) + (b * ua - a * ub))
        sa = sa + ((ta - pb) + ua * ja - ub * jb + beta * a)
        sb = sb + ((tb + pa) + ua * jb + ub * ja + beta * b)
        cw[k] = sw
        ch[0, k] = sa
        ch[1, k] = sb
        return sw, sa, sb

    lax.fori_loop(0, radii, wh_step, (zero, zero, zero))

    parts = [slice(2 * wide + i * half, 2 * wide + (i + 1) * half) for i in range(4)]
    w_at, ha_at, hb_at = parts[:3]
    own, over, under = slice(LAP, LAP + half), slice(LAP + 1, LAP + half + 1), slice(LAP - 1, LAP + half - 1)

    def at_b(s):
        return slice(s.start + wide, s.stop + wide)

    def compose(e, s):
        ca, cb = acc[own], acc[at_b(own)]
        ta, tb = theta(ca), theta(cb)
        pa = 0.5 * (acc[over] - acc[under])
        pb = 0.5 * (acc[at_b(over)] - acc[at_b(under)])
        a, b, ja, jb = (e[i * half:(i + 1) * half] for i in range(4))
        g, w, ha, hb = (s[p] for p in parts)
        n = float(radii)
        acc[w_at] += w + g * (ta + pb) + (b * ca - a * cb)
        acc[ha_at] += ha + n * (ta - pb) + (ca * ja - cb * jb)
        acc[hb_at] += hb + n * (tb + pa) + (ca * jb + cb * ja)
        acc[0:2 * wide] += s[0:2 * wide]

    def wait_seg(i):
        remote(seg_e.at[0], slot_e.at[i], e_send.at[i], e_recv.at[i], shell, patch).wait_recv()
        remote(seg_l.at[0], slot_s.at[i], s_send.at[i], s_recv.at[i], shell, patch).wait_recv()

    acc[...] = jnp.zeros_like(acc)
    for dz in range(chips - 1, 0, -1):
        @pl.when(chip >= dz)
        def _():
            for e in range(2):
                i = (dz - 1) * 2 + e
                wait_seg(i)
                compose(slot_e.at[i], slot_s.at[i])

    forward = remote(fsrc, fslot, f_sem.at[0], f_sem.at[1], partner, patch)

    @pl.when(core == 0)
    def _():
        pre[0] = acc[...]
        compose(seg_e.at[0], seg_l.at[0])
        fsrc[...] = acc[...]
        forward.start()
        forward.wait_recv()
        pre[1] = fslot[...]

    @pl.when(core == 1)
    def _():
        fsrc[...] = acc[...]
        forward.start()
        last = 2 * (chips - 1)
        wait_seg(last)
        compose(slot_e.at[last], slot_s.at[last])
        pre[1] = acc[...]
        forward.wait_recv()
        pre[0] = fslot[...]

    for copy in (j_left, j_right, b_left, b_right, forward):
        copy.wait_send()

    @pl.when(shell > 0)
    def _():
        remote(j_hbm.at[:, 0], jnext, rad_sem.at[0], rad_sem.at[1], shell - 1, patch).wait_send()

    for d in range(1, shells):
        @pl.when(shell + d < shells)
        def _():
            for copy in b_copies(d):
                copy.wait_send()

    for group in ((seg_e, slot_e, e_send, e_recv), (seg_l, slot_s, s_send, s_recv)):
        @pl.when(core == 0)
        def _():
            own_copy(*group).wait_send()

        for dz in range(1, chips):
            @pl.when(chip + dz < chips)
            def _():
                for copy in seg_copies(dz, *group):
                    copy.wait_send()


def tail(step, jp, up, bfin, gs, barj, cw, ch, pre, beta_out, u_out, w_out, h_out, uv, wv, hv, sems):
    radii, cols, lanes = cw.shape
    half = cols // 2
    wide = half + 2 * LAP
    inner = slice(PAD, PAD + cols)
    theta = make_theta(lanes)
    copies = [pltpu.make_async_copy(bfin, beta_out, sems.at[0, 0])]
    copies[0].start()

    def rows(at, n):
        return jnp.concatenate([pre[0, at:at + n], pre[1, at:at + n]], axis=0)

    ca, cb = rows(LAP, half), rows(wide + LAP, half)
    ta, tb = theta(ca), theta(cb)
    pa = 0.5 * (rows(LAP + 1, half) - rows(LAP - 1, half))
    pb = 0.5 * (rows(wide + LAP + 1, half) - rows(wide + LAP - 1, half))
    re_bar, eth_a, eth_b = ta + pb, ta - pb, tb + pa
    sq = step * step

    def final(k, carry):
        dw, da, db = carry
        a, b = jp[0, k, inner], jp[1, k, inner]
        ja, jb = barj[0, k], barj[1, k]
        dw = dw + (gs[k] * re_bar + (b * ca - a * cb))
        da = da + (eth_a + (ca * ja - cb * jb))
        db = db + (eth_b + (ca * jb + cb * ja))
        uv[0, k] = step * (up[0, k, inner] + ca)
        uv[1, k] = step * (up[1, k, inner] + cb)
        wv[k] = sq * (cw[k] + dw)
        hv[0, k] = sq * (ch[0, k] + da)
        hv[1, k] = sq * (ch[1, k] + db)
        return dw, da, db

    carry = tuple(rows(2 * wide + i * half, half) for i in range(3))
    chunks = sems.shape[1]
    size = radii // chunks
    for i in range(chunks):
        carry = lax.fori_loop(i * size, (i + 1) * size, final, carry, unroll=2)
        at = pl.ds(i * size, size)
        more = [pltpu.make_async_copy(uv.at[:, at], u_out.at[:, at], sems.at[1, i]),
                pltpu.make_async_copy(wv.at[at], w_out.at[at], sems.at[2, i]),
                pltpu.make_async_copy(hv.at[:, at], h_out.at[:, at], sems.at[3, i])]
        for copy in more:
            copy.start()
        copies += more
    for copy in copies:
        copy.wait()


def solution(mesh):
    shells, patches = mesh.shape["shell"], mesh.shape["patch"]
    chips = shells // 2

    def local(field_j):
        _, radii, cols, lanes = field_j.shape
        step = 1.0 / math.sqrt(radii * shells)
        f32 = jnp.float32
        vm = lambda *s: pltpu.VMEM(s, f32)
        tall = cols + 2 * PAD
        half = cols // 2
        wide = half + 2 * LAP
        late, early, state = 2 * wide + 4 * half, 4 * half, 2 * wide + 3 * half
        segs = 2 * (chips - 1) + 1
        outer = shells - 1
        dma = pltpu.SemaphoreType.DMA
        scratch = [
            vm(radii, tall, lanes), vm(radii, tall, lanes), vm(radii, tall, lanes), vm(2, cols, lanes),
            vm(2, 2, radii, lanes), vm(2, 2, radii, lanes), vm(2, 2, radii, lanes), vm(2, 2, radii, lanes),
            vm(cols, lanes), vm(outer, cols, lanes), vm(outer, 8, lanes), vm(outer, 8, lanes),
            vm(tall, lanes), vm(2, tall, lanes),
            vm(2, early, lanes), vm(2, late, lanes), vm(segs, early, lanes), vm(segs, late, lanes),
            vm(state, lanes), vm(state, lanes), vm(state, lanes),
            dma, dma((2,)), dma((2,)), dma((2,)), dma((2,)), dma((2,)),
            dma((3, outer)), dma((3, outer)), dma((segs,)), dma((segs,)), dma((segs,)), dma((segs,)), dma((2,)),
        ]
        shape = lambda *s: jax.ShapeDtypeStruct(s, f32)
        vmem = pl.BlockSpec(memory_space=pltpu.VMEM)
        hbm = pl.BlockSpec(memory_space=pltpu.HBM)
        plain, pair = (radii, cols, lanes), (2, radii, cols, lanes)
        padded = (2, radii, tall, lanes)
        found = pl.pallas_call(
            functools.partial(kernel, shells, patches, step),
            out_shape=(shape(*padded), shape(*padded), shape(*plain), shape(*plain), shape(*pair),
                       shape(*plain), shape(*pair), shape(2, state, lanes)),
            in_specs=[hbm],
            out_specs=(vmem,) * 8,
            scratch_shapes=scratch,
            compiler_params=pltpu.CompilerParams(
                collective_id=0, has_side_effects=True, vmem_limit_bytes=28 * 1024 * 1024),
        )(pltpu.with_memory_space_constraint(field_j, pltpu.HBM))
        return pl.pallas_call(
            functools.partial(tail, step),
            out_shape=(shape(*plain), shape(*pair), shape(*plain), shape(*pair)),
            in_specs=[vmem] * 8,
            out_specs=(hbm,) * 4,
            scratch_shapes=[vm(*pair), vm(*plain), vm(*pair), dma((4, 4))],
            compiler_params=pltpu.CompilerParams(vmem_limit_bytes=28 * 1024 * 1024),
        )(*found)

    return jax.shard_map(
        local,
        mesh=mesh,
        in_specs=(P(None, "shell", "patch", None),),
        out_specs=(
            P("shell", "patch", None),
            P(None, "shell", "patch", None),
            P("shell", "patch", None),
            P(None, "shell", "patch", None),
        ),
        check_vma=False,
    )
```

time: 32.1 us -> 34.5 us (1.075)
  the two profiles are of different devices: /device:TPU:25 before, /device:TPU:17 now
where the time goes in v1:
time: 34.5 us; the launch traced here: 34.3 us
  Pallas kernels  33.7 us (98%)
  between operations  0.64 us (2%)
    pallas_call x1, Pallas kernels, local(): pl.pallas_call(functools.partial(kernel, shells, patches, step), out_shap...  31.9 us
    pallas_call x1, Pallas kernels, local(): pl.pallas_call(functools.partial(tail, step), out_shape=(shape(*plain), s...  1.83 us

profile of v1, /device:TPU:17, one launch (start us, length us, event | category | flops | bytes accessed | tf_op | source)
XLA Modules:
  0.0 34.3 jit_solution(6195571213492345742)
XLA Ops:
  0.6 31.9 %shard_map.46 = (f32[2,32,48,128]{3,2,1,0:T(8,128)S(1)}, f32[2,32,48,128]{3,2,1,0:T(8,128)S(1)}, f32[32,32,128]{2,1,0:T(8,128)S(1)}, f32[32,32,128]{2,1,0:T(8,12...) custom-call(f32[2,32,32,128]{3,2,1,0:T(8,128)} %j_hbm.1), custom_call_target="tpu_custom_call" | custom-call | tf_op jit(solution)/shard_map/pallas_call | solution.py:485
  32.5 1.8 %shard_map.47 = (f32[32,32,128]{2,1,0:T(8,128)}, f32[2,32,32,128]{3,2,1,0:T(8,128)}, f32[32,32,128]{2,1,0:T(8,128)}, f32[2,32,32,128]{3,2,1,0:T(8,128)}) custom-call(f32[2,32,48,128]{3,2,1,0:T(8,128)S(1)} %get-tuple-element.12.jp, f32[2,32,48,128]{3,2,1,0:T(8,128)S(1)} %get-tuple-element.13.up, f32[32,32,128]{2,1,0:T(8,128)S(1)} %get-tuple-element.14.bfin, ...), custom_call_target="tpu_custom_call" | custom-call | tf_op jit(solution)/shard_map/pallas_call | solution.py:495

commit v2 on v0

v2 whole, which is shorter than its diff:
```python
import functools
import math

import jax
import jax.numpy as jnp
from jax import lax
from jax.experimental import pallas as pl
from jax.experimental.pallas import tpu as pltpu
from jax.sharding import PartitionSpec as P

PAD = 8


def remote(src, dst, send_sem, recv_sem, shell, patch):
    return pltpu.make_async_remote_copy(
        src_ref=src,
        dst_ref=dst,
        send_sem=send_sem,
        recv_sem=recv_sem,
        device_id=(shell, patch),
        device_id_type=pl.DeviceIdType.MESH,
    )


def make_theta(lanes):
    lane = lax.broadcasted_iota(jnp.int32, (8, lanes), 1)
    keep_f = jnp.where(lane == lanes - 1, 0.0, 0.5).astype(jnp.float32)
    keep_b = jnp.where(lane == 0, 0.0, 0.5).astype(jnp.float32)

    def theta(x):
        reps = x.shape[0] // 8
        mf = jnp.concatenate([keep_f] * reps, axis=0) if reps > 1 else keep_f
        mb = jnp.concatenate([keep_b] * reps, axis=0) if reps > 1 else keep_b
        return pltpu.roll(x, lanes - 1, 1) * mf - pltpu.roll(x, 1, 1) * mb

    return theta


def whole(edges, middle, f, k):
    return jnp.concatenate([edges[0, f, k], middle[f, k], edges[1, f, k]], axis=0)


def eth_planes(theta, pair, inner, above, below):
    ta, tb = theta(pair[0, inner]), theta(pair[1, inner])
    pa = 0.5 * (pair[0, above] - pair[0, below])
    pb = 0.5 * (pair[1, above] - pair[1, below])
    return ta + pb, ta - pb, tb + pa


def beta_point(theta, jp, k, lo, n, next_a, next_b):
    at = slice(PAD + lo, PAD + lo + n)
    up1 = slice(PAD + lo + 1, PAD + lo + n + 1)
    dn1 = slice(PAD + lo - 1, PAD + lo + n - 1)
    a, b = jp[0, k, at], jp[1, k, at]
    ra, rb = next_a - a, next_b - b
    ta, tb = theta(a), theta(b)
    pa = 0.5 * (jp[0, k, up1] - jp[0, k, dn1])
    pb = 0.5 * (jp[1, k, up1] - jp[1, k, dn1])
    ea, eb = ta - pb, tb + pa
    return 0.25 * (0.5 * (ra * ra + rb * rb) - (ea * ea + eb * eb)), ta + pb, tb - pa


def gather(shells, patches, j_hbm, jp, jnext, b_in, barj_in, jnear, jedge, jhalo, load_sem, rad_sem, jh_send, jh_recv):
    radii, cols, lanes = jp.shape[1], jp.shape[2] - 2 * PAD, jp.shape[3]
    shell, patch = lax.axis_index("shell"), lax.axis_index("patch")
    right = lax.rem(patch + 1, patches)
    left = lax.rem(patch + patches - 1, patches)
    inner = slice(PAD, PAD + cols)
    before, after = slice(PAD - 1, PAD), slice(PAD + cols, PAD + cols + 1)
    theta = make_theta(lanes)

    load = pltpu.make_async_copy(j_hbm, jp.at[:, :, pl.ds(PAD, cols), :], load_sem)
    load.start()
    barrier = pltpu.get_barrier_semaphore()
    for p in (left, right):
        pl.semaphore_signal(barrier, inc=1, device_id=(shell, p), device_id_type=pl.DeviceIdType.MESH)

    @pl.when(shell > 0)
    def _():
        pl.semaphore_signal(barrier, inc=1, device_id=(shell - 1, patch), device_id_type=pl.DeviceIdType.MESH)

    @pl.when(shell < shells - 1)
    def _():
        pl.semaphore_signal(barrier, inc=1, device_id=(shell + 1, patch), device_id_type=pl.DeviceIdType.MESH)

    load.wait()

    def pack(k, c):
        for f in range(2):
            jedge[0, f, pl.ds(k, 1), :] = jp[f, k, PAD:PAD + 1, :]
            jedge[1, f, pl.ds(k, 1), :] = jp[f, k, PAD + cols - 1:PAD + cols, :]
        return c

    lax.fori_loop(0, radii, pack, 0, unroll=8)
    pl.semaphore_wait(barrier, 2 + (shell > 0).astype(jnp.int32) + (shell < shells - 1).astype(jnp.int32))
    to_left = remote(jedge.at[0], jhalo.at[1], jh_send.at[0], jh_recv.at[1], shell, left)
    to_right = remote(jedge.at[1], jhalo.at[0], jh_send.at[1], jh_recv.at[0], shell, right)
    to_left.start()
    to_right.start()

    def down(there):
        return remote(j_hbm.at[:, 0], jnear, rad_sem.at[0], rad_sem.at[1], there, patch)

    @pl.when(shell > 0)
    def _():
        down(shell - 1).start()

    lo, n = 8, cols - 16

    def keep(k, found, total):
        source, ja, jb = found
        barj_in[0, k], barj_in[1, k] = ja, jb
        b_in[k] = total + source
        return total + source

    def beta_step(k, total):
        at = slice(PAD + lo, PAD + lo + n)
        return keep(k, beta_point(theta, jp, k, lo, n, jp[0, k + 1, at], jp[1, k + 1, at]), total)

    total = lax.fori_loop(0, radii - 1, beta_step, jnp.zeros((n, lanes), jnp.float32), unroll=2)

    @pl.when(shell == shells - 1)
    def _():
        for f in range(2):
            jnext[f] = jp[f, radii - 1, inner]

    @pl.when(shell < shells - 1)
    def _():
        down(shell).wait_recv()
        jnext[...] = jnear[...]

    keep(radii - 1, beta_point(theta, jp, radii - 1, lo, n, jnext[0, lo:lo + n], jnext[1, lo:lo + n]), total)
    to_left.wait_recv()
    to_right.wait_recv()

    def unpack(k, c):
        for f in range(2):
            jp[f, k, before, :] = jhalo[0, f, pl.ds(k, 1), :]
            jp[f, k, after, :] = jhalo[1, f, pl.ds(k, 1), :]
        return c

    lax.fori_loop(0, radii, unpack, 0, unroll=8)
    to_left.wait_send()
    to_right.wait_send()

    @pl.when(shell > 0)
    def _():
        down(shell - 1).wait_send()


def kernel(shells, patches, step, jp, jnext, b_in, barj_in, up, bfin, gs, cw, ch, ct, below_h, barj_e,
           bp, es, dr, bt, bedge, bhalo, below_b, below_u,
           sum_b, part_b, tot_b, slot_b, pre_b,
           sum_u, part_u, tot_u, slot_u, pre_u,
           sum_h, part_h, tot_h, slot_h, pre_h,
           rim_b, rtot_b, rpart_b, rslot_b, rim_u, rtot_u, rpart_u, rslot_u,
           edge_send, edge_recv, part_sem, send_sem, recv_sem, fwd_sem,
           rpart_send, rpart_recv, rim_send, rim_recv):
    radii, cols, lanes = cw.shape
    tall = cols + 8
    f32 = jnp.float32
    chips = shells // 2
    shell, patch = lax.axis_index("shell"), lax.axis_index("patch")
    chip, core = shell // 2, shell % 2
    partner = shell + 1 - 2 * core
    right = lax.rem(patch + 1, patches)
    left = lax.rem(patch + patches - 1, patches)
    inner = slice(PAD, PAD + cols)
    above = slice(PAD + 1, PAD + cols + 1)
    below = slice(PAD - 1, PAD + cols - 1)
    theta = make_theta(lanes)

    barrier = pltpu.get_barrier_semaphore()
    for d in range(shells):
        there = lax.rem(shell + d, shells)
        for p in (patch, left, right):
            if d == 0 and p is patch:
                continue
            pl.semaphore_signal(barrier, inc=1, device_id=(there, p),
                                device_id_type=pl.DeviceIdType.MESH)

    spans = ((0, 0), (1, cols - 8))

    def edge_step(k, next_of, totals):
        new = []
        for (side, lo), total in zip(spans, totals):
            source, ja, jb = beta_point(theta, jp, k, lo, 8, next_of(0, k, lo), next_of(1, k, lo))
            barj_e[side, 0, k], barj_e[side, 1, k] = ja, jb
            total = total + source
            bp[k, PAD + lo:PAD + lo + 8] = total
            at = 6 * side
            bedge[side, 0, pl.ds(k, 1), :] = total[at:at + 1]
            bedge[side, 1, pl.ds(k, 1), :] = total[at + 1:at + 2]
            new.append(total)
        return tuple(new)

    zero8 = jnp.zeros((8, lanes), f32)
    totals = lax.fori_loop(
        0, radii - 1, lambda k, t: edge_step(k, lambda f, k, lo: jp[f, k + 1, PAD + lo:PAD + lo + 8], t),
        (zero8, zero8), unroll=2)
    totals = edge_step(radii - 1, lambda f, k, lo: jnext[f, lo:lo + 8], totals)
    sum_b[0:8] = totals[0]
    sum_b[8:cols - 8] = b_in[radii - 1]
    sum_b[cols - 8:] = totals[1]

    def pieces(stage, own, part, tot, slots, both):
        half = own.shape[0] // 2
        mine = pl.ds(pl.multiple_of(core * half, 8), half)
        first = remote(own, part, part_sem.at[stage, 0], part_sem.at[stage, 1], partner, patch)
        sends = []
        for d in range(1, chips):
            if both:
                sends.append([
                    remote(tot.at[mine], slots.at[d - 1, mine], send_sem.at[stage, d - 1, e],
                           recv_sem.at[stage, d - 1, core], (chip + d) * 2 + e, patch)
                    for e in range(2)])
            else:
                sends.append([
                    remote(tot.at[mine], slots.at[d - 1, mine], send_sem.at[stage, d - 1, 0],
                           recv_sem.at[stage, d - 1, 0], (chip + d) * 2 + core, patch)])
        return mine, half, first, sends

    def rim_pieces(stage, rim, rtot, rpart, rslot):
        over = left * (1 - core) + right * core
        near = [
            remote(rim.at[0], rpart.at[1], rpart_send.at[stage, 0], rpart_recv.at[stage, 1], partner, left),
            remote(rim.at[1], rpart.at[0], rpart_send.at[stage, 1], rpart_recv.at[stage, 0], partner, right)]
        far = [[
            remote(rtot.at[core], rslot.at[d - 1, 1 - core], rim_send.at[stage, d - 1, e],
                   rim_recv.at[stage, d - 1, 1 - core], (chip + d) * 2 + e, over)
            for e in range(2)] for d in range(1, chips)]
        return near, far

    def begin(stage, own, part, tot, slots, both, rims=None, lines=None):
        mine, half, first, sends = pieces(stage, own, part, tot, slots, both)
        first.start()
        if rims is not None:
            rim, rtot, rpart, rslot = rims
            for side in range(2):
                for i, r in enumerate(lines[side]):
                    rim[side, i:i + 1] = own[r:r + 1]
            near, far = rim_pieces(stage, rim, rtot, rpart, rslot)

            @pl.when(core == 0)
            def _():
                for copy in near:
                    copy.start()

        first.wait_recv()
        tot[mine] = own[mine] + part[mine]
        if rims is not None:
            for side in range(2):
                for i, r in enumerate(lines[side]):
                    rtot[side, i:i + 1] = own[r:r + 1] + part[r:r + 1]
        for d in range(1, chips):
            @pl.when(chip + d < chips)
            def _():
                for copy in sends[d - 1]:
                    copy.start()
                if rims is not None:
                    for copy in far[d - 1]:
                        copy.start()

    def end(stage, own, part, tot, slots, pre, out, both, rims=None):
        mine, half, first, sends = pieces(stage, own, part, tot, slots, both)
        if rims is not None:
            rim, rtot, rpart, rslot = rims
            near, far = rim_pieces(stage, rim, rtot, rpart, rslot)

        @pl.when(core == 0)
        def _():
            out[...] = jnp.zeros_like(out)

        @pl.when(core == 1)
        def _():
            out[...] = part[...]
            if rims is not None:
                for copy in near:
                    copy.wait_recv()

        if rims is not None:
            @pl.when(core == 0)
            def _():
                rpart[...] = jnp.zeros_like(rpart)

        if both:
            for d in range(1, chips):
                @pl.when(chip >= d)
                def _():
                    for e in range(2):
                        piece = pl.ds(e * half, half)
                        remote(tot.at[piece], slots.at[d - 1, piece], send_sem.at[stage, d - 1, e],
                               recv_sem.at[stage, d - 1, e], shell, patch).wait_recv()
                    out[...] += slots[d - 1]
        else:
            @pl.when(chip > 0)
            def _():
                pre[mine] = jnp.zeros((half, lanes), f32)

            for d in range(1, chips):
                @pl.when(chip >= d)
                def _():
                    for copy in sends[d - 1]:
                        copy.wait_recv()
                    pre[mine] += slots[d - 1, mine]

            @pl.when(chip > 0)
            def _():
                fwd = remote(pre.at[mine], pre.at[mine], fwd_sem.at[stage, 0], fwd_sem.at[stage, 1],
                             partner, patch)
                fwd.start()
                fwd.wait_recv()
                out[...] += pre[...]

        if rims is not None:
            for d in range(1, chips):
                @pl.when(chip >= d)
                def _():
                    for e in range(2):
                        remote(rtot.at[e], rslot.at[d - 1, e], rim_send.at[stage, d - 1, 0],
                               rim_recv.at[stage, d - 1, e], shell, patch).wait_recv()
                    rpart[...] += rslot[d - 1]

    def finish(stage, own, part, tot, slots, pre, both, rims=None):
        mine, half, first, sends = pieces(stage, own, part, tot, slots, both)
        first.wait_send()
        if rims is not None:
            near, far = rim_pieces(stage, *rims)

            @pl.when(core == 0)
            def _():
                for copy in near:
                    copy.wait_send()

        for d in range(1, chips):
            @pl.when(chip + d < chips)
            def _():
                for copy in sends[d - 1]:
                    copy.wait_send()
                if rims is not None:
                    for copy in far[d - 1]:
                        copy.wait_send()

        if not both:
            @pl.when(chip > 0)
            def _():
                remote(pre.at[mine], pre.at[mine], fwd_sem.at[stage, 0], fwd_sem.at[stage, 1],
                       partner, patch).wait_send()

    pl.semaphore_wait(barrier, 3 * shells - 1)
    b_left = remote(bedge.at[0], bhalo.at[1], edge_send.at[0], edge_recv.at[1], shell, left)
    b_right = remote(bedge.at[1], bhalo.at[0], edge_send.at[1], edge_recv.at[0], shell, right)
    b_left.start()
    b_right.start()
    rims_b = (rim_b, rtot_b, rpart_b, rslot_b)
    begin(0, sum_b, part_b, tot_b, slot_b, True, rims_b, ((0, 1), (cols - 2, cols - 1)))

    zero = jnp.zeros((cols, lanes), f32)

    def local_step(k, carry):
        se, sa, sb, sja, sjb, sba, sbb = carry
        bp[k, PAD + 8:PAD + cols - 8] = b_in[k]
        beta = jnp.concatenate([bp[k, PAD:PAD + 8], b_in[k], bp[k, PAD + cols - 8:PAD + cols]], axis=0)
        grow = jnp.exp((2.0 * step) * beta)
        es[k, inner] = grow
        dr[k, inner] = theta(beta)
        a, b = jp[0, k, inner], jp[1, k, inner]
        ja, jb = whole(barj_e, barj_in, 0, k), whole(barj_e, barj_in, 1, k)
        return (se + grow, sa + a, sb + b, sja + ja, sjb + jb, sba + beta * a, sbb + beta * b)

    se, sa, sb, sja, sjb, sba, sbb = lax.fori_loop(0, radii, local_step, (zero,) * 7, unroll=2)
    b_left.wait_recv()
    b_right.wait_recv()

    def halo_step(k, c):
        for i in range(2):
            bp[k, PAD - 2 + i:PAD - 1 + i, :] = bhalo[0, i, pl.ds(k, 1), :]
            bp[k, PAD + cols + i:PAD + cols + i + 1, :] = bhalo[1, i, pl.ds(k, 1), :]
        return c

    lax.fori_loop(0, radii, halo_step, 0, unroll=8)

    def halo_exp(k, c):
        for lo in (0, PAD + cols):
            x = bp[k, lo:lo + 8]
            es[k, lo:lo + 8] = jnp.exp((2.0 * step) * x)
            dr[k, lo:lo + 8] = theta(x)
        return c

    lax.fori_loop(0, radii, halo_exp, 0, unroll=4)
    bt[...] = jnp.zeros_like(bt)
    end(0, sum_b, part_b, tot_b, slot_b, pre_b, below_b, True, rims_b)
    bt[inner] = below_b[...]
    bt[PAD - 2:PAD] = rpart_b[0]
    bt[PAD + cols:PAD + cols + 2] = rpart_b[1]

    first = PAD - 1
    mid, hi, lo = slice(first, first + tall), slice(first + 1, first + tall + 1), slice(first - 1, first + tall - 1)
    base_r = theta(bt[mid])
    base_i = bt[hi] - bt[lo]
    base_g = step * jnp.exp((2.0 * step) * bt[mid])
    wide_zero = jnp.zeros((tall, lanes), f32)

    def u_step(k, carry):
        ua, ub = carry
        growth = base_g * es[k, mid]
        br = dr[k, mid] + base_r
        bi = 0.5 * ((bp[k, hi] - bp[k, lo]) + base_i)
        a, b = jp[0, k, mid], jp[1, k, mid]
        ua = ua + growth * (br - (a * br + b * bi))
        ub = ub + growth * (bi - (b * br - a * bi))
        up[0, k, mid] = ua
        up[1, k, mid] = ub
        return ua, ub

    ua_sum, ub_sum = lax.fori_loop(0, radii, u_step, (wide_zero, wide_zero), unroll=2)
    sum_u[:cols] = ua_sum[1:cols + 1]
    sum_u[cols:] = ub_sum[1:cols + 1]
    rims_u = (rim_u, rtot_u, rpart_u, rslot_u)
    begin(1, sum_u, part_u, tot_u, slot_u, False, rims_u, ((0, cols), (cols - 1, 2 * cols - 1)))

    full_b = bt[inner]
    grow_b = jnp.exp((2.0 * step) * full_b)

    def wh_step(k, carry):
        sw, ha, hb = carry
        beta = bp[k, inner] + full_b
        growth = grow_b * es[k, inner]
        a, b = jp[0, k, inner], jp[1, k, inner]
        ua, ub = up[0, k, inner], up[1, k, inner]
        ta, tb = theta(ua), theta(ub)
        pa = 0.5 * (up[0, k, above] - up[0, k, below])
        pb = 0.5 * (up[1, k, above] - up[1, k, below])
        ja, jb = whole(barj_e, barj_in, 0, k), whole(barj_e, barj_in, 1, k)
        sw = sw + (growth * (ta + pb) + (b * ua - a * ub))
        ha = ha + ((ta - pb) + ua * ja - ub * jb + beta * a)
        hb = hb + ((tb + pa) + ua * jb + ub * ja + beta * b)
        cw[k] = sw
        ch[0, k] = ha
        ch[1, k] = hb
        return sw, ha, hb

    sw, ha, hb = lax.fori_loop(0, radii, wh_step, (zero, zero, zero))
    end(1, sum_u, part_u, tot_u, slot_u, pre_u, below_u, False, rims_u)
    for f in range(2):
        ct[f] = jnp.zeros(ct.shape[1:], f32)
        ct[f, inner] = below_u[f * cols:(f + 1) * cols]
        ct[f, PAD - 1:PAD] = rpart_u[0, f:f + 1]
        ct[f, PAD + cols:PAD + cols + 1] = rpart_u[1, f:f + 1]
    ca, cb = ct[0, inner], ct[1, inner]
    re_bar, eth_a, eth_b = eth_planes(theta, ct, inner, above, below)
    n = float(radii)
    sum_h[:cols] = sw + (grow_b * se) * re_bar + (sb * ca - sa * cb)
    sum_h[cols:2 * cols] = ha + n * eth_a + (ca * sja - cb * sjb)
    sum_h[2 * cols:] = hb + n * eth_b + (ca * sjb + cb * sja)
    begin(2, sum_h, part_h, tot_h, slot_h, False)

    def fields_step(k, c):
        bfin[k] = step * (bp[k, inner] + full_b)
        gs[k] = grow_b * es[k, inner]
        return c

    lax.fori_loop(0, radii, fields_step, 0, unroll=2)
    end(2, sum_h, part_h, tot_h, slot_h, pre_h, below_h, False)
    b_left.wait_send()
    b_right.wait_send()
    finish(0, sum_b, part_b, tot_b, slot_b, pre_b, True, rims_b)
    finish(1, sum_u, part_u, tot_u, slot_u, pre_u, False, rims_u)
    finish(2, sum_h, part_h, tot_h, slot_h, pre_h, False)


def tail(step, jp, barj_in, barj_e, up, bfin, gs, cw, ch, ct, below_h, beta_out, u_out, w_out, h_out, uv, wv, hv, sems):
    radii, cols, lanes = cw.shape
    inner = slice(PAD, PAD + cols)
    above = slice(PAD + 1, PAD + cols + 1)
    below = slice(PAD - 1, PAD + cols - 1)
    theta = make_theta(lanes)
    copies = [pltpu.make_async_copy(bfin, beta_out, sems.at[0, 0])]
    copies[0].start()
    ca, cb = ct[0, inner], ct[1, inner]
    re_bar, eth_a, eth_b = eth_planes(theta, ct, inner, above, below)
    sq = step * step

    def final(k, carry):
        dw, da, db = carry
        a, b = jp[0, k, inner], jp[1, k, inner]
        ja, jb = whole(barj_e, barj_in, 0, k), whole(barj_e, barj_in, 1, k)
        dw = dw + (gs[k] * re_bar + (b * ca - a * cb))
        da = da + (eth_a + (ca * ja - cb * jb))
        db = db + (eth_b + (ca * jb + cb * ja))
        uv[0, k] = step * (up[0, k, inner] + ca)
        uv[1, k] = step * (up[1, k, inner] + cb)
        wv[k] = sq * (cw[k] + dw)
        hv[0, k] = sq * (ch[0, k] + da)
        hv[1, k] = sq * (ch[1, k] + db)
        return dw, da, db

    carry = tuple(below_h[i * cols:(i + 1) * cols] for i in range(3))
    chunks = sems.shape[1]
    size = radii // chunks
    for i in range(chunks):
        carry = lax.fori_loop(i * size, (i + 1) * size, final, carry, unroll=2)
        at = pl.ds(i * size, size)
        more = [pltpu.make_async_copy(uv.at[:, at], u_out.at[:, at], sems.at[1, i]),
                pltpu.make_async_copy(wv.at[at], w_out.at[at], sems.at[2, i]),
                pltpu.make_async_copy(hv.at[:, at], h_out.at[:, at], sems.at[3, i])]
        for copy in more:
            copy.start()
        copies += more
    for copy in copies:
        copy.wait()


def solution(mesh):
    shells, patches = mesh.shape["shell"], mesh.shape["patch"]
    chips = shells // 2

    def local(field_j):
        _, radii, cols, lanes = field_j.shape
        step = 1.0 / math.sqrt(radii * shells)
        f32 = jnp.float32
        vm = lambda *s: pltpu.VMEM(s, f32)
        shape = lambda *s: jax.ShapeDtypeStruct(s, f32)
        tall = cols + 2 * PAD
        dma = pltpu.SemaphoreType.DMA
        vmem = pl.BlockSpec(memory_space=pltpu.VMEM)
        hbm = pl.BlockSpec(memory_space=pltpu.HBM)
        plain, pair = (radii, cols, lanes), (2, radii, cols, lanes)
        padded, middle = (2, radii, tall, lanes), (radii, cols - 16, lanes)
        limit = 24 * 1024 * 1024
        jp, jnext, b_in, barj_in = pl.pallas_call(
            functools.partial(gather, shells, patches),
            out_shape=(shape(*padded), shape(2, cols, lanes), shape(*middle), shape(2, *middle)),
            in_specs=[hbm],
            out_specs=(vmem,) * 4,
            scratch_shapes=[vm(2, cols, lanes), vm(2, 2, radii, lanes), vm(2, 2, radii, lanes),
                            dma, dma((2,)), dma((2,)), dma((2,))],
            compiler_params=pltpu.CompilerParams(
                collective_id=0, has_side_effects=True, vmem_limit_bytes=limit),
        )(pltpu.with_memory_space_constraint(field_j, pltpu.HBM))

        many = max(chips - 1, 1)
        scratch = [vm(radii, tall, lanes)] * 3 + [vm(tall, lanes), vm(2, 2, radii, lanes), vm(2, 2, radii, lanes),
                                                  vm(cols, lanes), vm(2 * cols, lanes)]
        for n in (1, 2, 3):
            scratch += [vm(n * cols, lanes)] * 3 + [vm(many, n * cols, lanes), vm(n * cols, lanes)]
        for _ in range(2):
            scratch += [vm(2, 2, lanes)] * 3 + [vm(many, 2, 2, lanes)]
        scratch += [dma((2,)), dma((2,)), dma((3, 2)), dma((3, many, 2)), dma((3, many, 2)), dma((3, 2)),
                    dma((2, 2)), dma((2, 2)), dma((2, many, 2)), dma((2, many, 2))]
        up, bfin, gs, cw, ch, ct, below_h, barj_e = pl.pallas_call(
            functools.partial(kernel, shells, patches, step),
            out_shape=(shape(*padded), shape(*plain), shape(*plain), shape(*plain), shape(*pair),
                       shape(2, tall, lanes), shape(3 * cols, lanes), shape(2, 2, radii, 8, lanes)),
            in_specs=[vmem] * 4,
            out_specs=(vmem,) * 8,
            scratch_shapes=scratch,
            compiler_params=pltpu.CompilerParams(
                collective_id=1, has_side_effects=True, vmem_limit_bytes=limit),
        )(jp, jnext, b_in, barj_in)
        return pl.pallas_call(
            functools.partial(tail, step),
            out_shape=(shape(*plain), shape(*pair), shape(*plain), shape(*pair)),
            in_specs=[vmem] * 10,
            out_specs=(hbm,) * 4,
            scratch_shapes=[vm(*pair), vm(*plain), vm(*pair), dma((4, 4))],
            compiler_params=pltpu.CompilerParams(vmem_limit_bytes=limit),
        )(jp, barj_in, barj_e, up, bfin, gs, cw, ch, ct, below_h)

    return jax.shard_map(
        local,
        mesh=mesh,
        in_specs=(P(None, "shell", "patch", None),),
        out_specs=(
            P("shell", "patch", None),
            P(None, "shell", "patch", None),
            P("shell", "patch", None),
            P(None, "shell", "patch", None),
        ),
        check_vma=False,
    )
```

time: 32.1 us -> 28.9 us (0.900)
  Pallas kernels: 31.3 us -> 28.1 us
    pallas_call x1, Pallas kernels: 29.6 us -> 21 us  [local(): pl.pallas_call(functools.partial(kernel, shells, patches, step), out_shap...]
    pallas_call x1 -> x2, Pallas kernels: 1.73 us -> 7.08 us  [the longest x1 5.25 us: local(): pl.pallas_call(functools.partial(gather, shells, patches), out_shape=(sha...]
where the time goes in v2:
time: 28.9 us; the launch traced here: 28.7 us
  Pallas kernels  28.1 us (97%)
  between operations  0.65 us (2%)
    pallas_call x1, Pallas kernels, local(): pl.pallas_call(functools.partial(kernel, shells, patches, step), out_shap...  21 us
    pallas_call x1, Pallas kernels, local(): pl.pallas_call(functools.partial(gather, shells, patches), out_shape=(sha...  5.25 us
    pallas_call x1, Pallas kernels, local(): pl.pallas_call(functools.partial(tail, step), out_shape=(shape(*plain), s...  1.83 us

profile of v2, /device:TPU:25, one launch (start us, length us, event | category | flops | bytes accessed | tf_op | source)
XLA Modules:
  0.0 28.7 jit_solution(11980590535530600049)
XLA Ops:
  0.6 5.3 %shard_map.46 = (f32[2,32,48,128]{3,2,1,0:T(8,128)S(1)}, f32[2,32,128]{2,1,0:T(8,128)S(1)}, f32[32,16,128]{2,1,0:T(8,128)S(1)}, f32[2,32,16,128]{3,2,1,0:T(8,128)S(1)}) custom-call(f32[2,32,32,128]{3,2,1,0:T(8,128)} %j_hbm.1), custom_call_target="tpu_custom_call" | custom-call | tf_op jit(solution)/shard_map/pallas_call | solution.py:531
  5.9 21.0 %shard_map.47 = (f32[2,32,48,128]{3,2,1,0:T(8,128)S(1)}, f32[32,32,128]{2,1,0:T(8,128)S(1)}, f32[32,32,128]{2,1,0:T(8,128)S(1)}, f32[32,32,128]{2,1,0:T(8,128)S(...) custom-call(f32[2,32,48,128]{3,2,1,0:T(8,128)S(1)} %get-tuple-elemen, ...), custom_call_target="tpu_custom_call" | custom-call | tf_op jit(solution)/shard_map/pallas_call | solution.py:551
  26.9 1.8 %shard_map.48 = (f32[32,32,128]{2,1,0:T(8,128)}, f32[2,32,32,128]{3,2,1,0:T(8,128)}, f32[32,32,128]{2,1,0:T(8,128)}, f32[2,32,32,128]{3,2,1,0:T(8,128)}) custom-call(f32[2,32,48,128]{3,2,1,0:T(8,128)S(1)} %get-tuple-element.16.jp, f32[2,32,16,128]{3,2,1,0:T(8,128)S(1)} %get-tuple-element.17.barj_in, f32[2,2,32,8,128]{4,3,2,1,0:T(8,128)S(1)} %get-tuple-element.20.barj_e, ...), custom_call_target="tpu_custom_call" | custom-call | tf_op jit(solution)/shard_map/pallas_call | solution.py:561

commit v3 on v2

--- a/solution.py
+++ b/solution.py
@@ -36,10 +36,6 @@
     return theta
 
 
-def whole(edges, middle, f, k):
-    return jnp.concatenate([edges[0, f, k], middle[f, k], edges[1, f, k]], axis=0)
-
-
 def eth_planes(theta, pair, inner, above, below):
     ta, tb = theta(pair[0, inner]), theta(pair[1, inner])
     pa = 0.5 * (pair[0, above] - pair[0, below])
@@ -47,113 +43,20 @@
     return ta + pb, ta - pb, tb + pa
 
 
-def beta_point(theta, jp, k, lo, n, next_a, next_b):
-    at = slice(PAD + lo, PAD + lo + n)
-    up1 = slice(PAD + lo + 1, PAD + lo + n + 1)
-    dn1 = slice(PAD + lo - 1, PAD + lo + n - 1)
-    a, b = jp[0, k, at], jp[1, k, at]
+def beta_terms(theta, a, b, next_a, next_b, pa, pb):
     ra, rb = next_a - a, next_b - b
     ta, tb = theta(a), theta(b)
-    pa = 0.5 * (jp[0, k, up1] - jp[0, k, dn1])
-    pb = 0.5 * (jp[1, k, up1] - jp[1, k, dn1])
     ea, eb = ta - pb, tb + pa
     return 0.25 * (0.5 * (ra * ra + rb * rb) - (ea * ea + eb * eb)), ta + pb, tb - pa
 
 
-def gather(shells, patches, j_hbm, jp, jnext, b_in, barj_in, jnear, jedge, jhalo, load_sem, rad_sem, jh_send, jh_recv):
-    radii, cols, lanes = jp.shape[1], jp.shape[2] - 2 * PAD, jp.shape[3]
-    shell, patch = lax.axis_index("shell"), lax.axis_index("patch")
-    right = lax.rem(patch + 1, patches)
-    left = lax.rem(patch + patches - 1, patches)
-    inner = slice(PAD, PAD + cols)
-    before, after = slice(PAD - 1, PAD), slice(PAD + cols, PAD + cols + 1)
-    theta = make_theta(lanes)
-
-    load = pltpu.make_async_copy(j_hbm, jp.at[:, :, pl.ds(PAD, cols), :], load_sem)
-    load.start()
-    barrier = pltpu.get_barrier_semaphore()
-    for p in (left, right):
-        pl.semaphore_signal(barrier, inc=1, device_id=(shell, p), device_id_type=pl.DeviceIdType.MESH)
-
-    @pl.when(shell > 0)
-    def _():
-        pl.semaphore_signal(barrier, inc=1, device_id=(shell - 1, patch), device_id_type=pl.DeviceIdType.MESH)
-
-    @pl.when(shell < shells - 1)
-    def _():
-        pl.semaphore_signal(barrier, inc=1, device_id=(shell + 1, patch), device_id_type=pl.DeviceIdType.MESH)
-
-    load.wait()
-
-    def pack(k, c):
-        for f in range(2):
-            jedge[0, f, pl.ds(k, 1), :] = jp[f, k, PAD:PAD + 1, :]
-            jedge[1, f, pl.ds(k, 1), :] = jp[f, k, PAD + cols - 1:PAD + cols, :]
-        return c
-
-    lax.fori_loop(0, radii, pack, 0, unroll=8)
-    pl.semaphore_wait(barrier, 2 + (shell > 0).astype(jnp.int32) + (shell < shells - 1).astype(jnp.int32))
-    to_left = remote(jedge.at[0], jhalo.at[1], jh_send.at[0], jh_recv.at[1], shell, left)
-    to_right = remote(jedge.at[1], jhalo.at[0], jh_send.at[1], jh_recv.at[0], shell, right)
-    to_left.start()
-    to_right.start()
-
-    def down(there):
-        return remote(j_hbm.at[:, 0], jnear, rad_sem.at[0], rad_sem.at[1], there, patch)
-
-    @pl.when(shell > 0)
-    def _():
-        down(shell - 1).start()
-
-    lo, n = 8, cols - 16
-
-    def keep(k, found, total):
-        source, ja, jb = found
-        barj_in[0, k], barj_in[1, k] = ja, jb
-        b_in[k] = total + source
-        return total + source
-
-    def beta_step(k, total):
-        at = slice(PAD + lo, PAD + lo + n)
-        return keep(k, beta_point(theta, jp, k, lo, n, jp[0, k + 1, at], jp[1, k + 1, at]), total)
-
-    total = lax.fori_loop(0, radii - 1, beta_step, jnp.zeros((n, lanes), jnp.float32), unroll=2)
-
-    @pl.when(shell == shells - 1)
-    def _():
-        for f in range(2):
-            jnext[f] = jp[f, radii - 1, inner]
-
-    @pl.when(shell < shells - 1)
-    def _():
-        down(shell).wait_recv()
-        jnext[...] = jnear[...]
-
-    keep(radii - 1, beta_point(theta, jp, radii - 1, lo, n, jnext[0, lo:lo + n], jnext[1, lo:lo + n]), total)
-    to_left.wait_recv()
-    to_right.wait_recv()
-
-    def unpack(k, c):
-        for f in range(2):
-            jp[f, k, before, :] = jhalo[0, f, pl.ds(k, 1), :]
-            jp[f, k, after, :] = jhalo[1, f, pl.ds(k, 1), :]
-        return c
-
-    lax.fori_loop(0, radii, unpack, 0, unroll=8)
-    to_left.wait_send()
-    to_right.wait_send()
-
-    @pl.when(shell > 0)
-    def _():
-        down(shell - 1).wait_send()
-
-
-def kernel(shells, patches, step, jp, jnext, b_in, barj_in, up, bfin, gs, cw, ch, ct, below_h, barj_e,
-           bp, es, dr, bt, bedge, bhalo, below_b, below_u,
+def kernel(shells, patches, step, j_hbm, jp, barj, up, bfin, gs, cw, ch, ct, below_h,
+           bp, es, dr, bt, bedge, bhalo, below_b, below_u, jnext, jedge, jside, jhalo, rows_w,
            sum_b, part_b, tot_b, slot_b, pre_b,
            sum_u, part_u, tot_u, slot_u, pre_u,
            sum_h, part_h, tot_h, slot_h, pre_h,
            rim_b, rtot_b, rpart_b, rslot_b, rim_u, rtot_u, rpart_u, rslot_u,
+           load_sem, rad_sem, jh_send, jh_recv, up_ready, side_ready,
            edge_send, edge_recv, part_sem, send_sem, recv_sem, fwd_sem,
            rpart_send, rpart_recv, rim_send, rim_recv):
     radii, cols, lanes = cw.shape
@@ -168,40 +71,132 @@
     inner = slice(PAD, PAD + cols)
     above = slice(PAD + 1, PAD + cols + 1)
     below = slice(PAD - 1, PAD + cols - 1)
+    before, after = slice(PAD - 1, PAD), slice(PAD + cols, PAD + cols + 1)
     theta = make_theta(lanes)
+    mesh_id = pl.DeviceIdType.MESH
+
+    load = pltpu.make_async_copy(j_hbm, jp.at[:, :, pl.ds(PAD, cols), :], load_sem)
+    load.start()
 
     barrier = pltpu.get_barrier_semaphore()
-    for d in range(shells):
-        there = lax.rem(shell + d, shells)
-        for p in (patch, left, right):
-            if d == 0 and p is patch:
-                continue
-            pl.semaphore_signal(barrier, inc=1, device_id=(there, p),
-                                device_id_type=pl.DeviceIdType.MESH)
-
-    spans = ((0, 0), (1, cols - 8))
-
-    def edge_step(k, next_of, totals):
-        new = []
-        for (side, lo), total in zip(spans, totals):
-            source, ja, jb = beta_point(theta, jp, k, lo, 8, next_of(0, k, lo), next_of(1, k, lo))
-            barj_e[side, 0, k], barj_e[side, 1, k] = ja, jb
-            total = total + source
-            bp[k, PAD + lo:PAD + lo + 8] = total
-            at = 6 * side
-            bedge[side, 0, pl.ds(k, 1), :] = total[at:at + 1]
-            bedge[side, 1, pl.ds(k, 1), :] = total[at + 1:at + 2]
-            new.append(total)
-        return tuple(new)
-
-    zero8 = jnp.zeros((8, lanes), f32)
-    totals = lax.fori_loop(
-        0, radii - 1, lambda k, t: edge_step(k, lambda f, k, lo: jp[f, k + 1, PAD + lo:PAD + lo + 8], t),
-        (zero8, zero8), unroll=2)
-    totals = edge_step(radii - 1, lambda f, k, lo: jnext[f, lo:lo + 8], totals)
-    sum_b[0:8] = totals[0]
-    sum_b[8:cols - 8] = b_in[radii - 1]
-    sum_b[cols - 8:] = totals[1]
+    def greet(there, p):
+        pl.semaphore_signal(barrier, inc=1, device_id=(there, p), device_id_type=mesh_id)
+
+    greet(partner, patch)
+    greet(shell, left)
+    greet(shell, right)
+
+    @pl.when(chip > 0)
+    def _():
+        greet(shell - 2, patch)
+
+        @pl.when(core == 0)
+        def _():
+            greet(shell - 1, patch)
+
+    @pl.when(chip < chips - 1)
+    def _():
+        greet(shell + 2, patch)
+
+        @pl.when(core == 1)
+        def _():
+            greet(shell + 1, patch)
+
+    load.wait()
+
+    def pack(k, c):
+        for f in range(2):
+            jedge[0, f, pl.ds(k, 1), :] = jp[f, k, PAD:PAD + 1, :]
+            jedge[1, f, pl.ds(k, 1), :] = jp[f, k, PAD + cols - 1:PAD + cols, :]
+        return c
+
+    lax.fori_loop(0, radii, pack, 0, unroll=8)
+    inside, outside = (chip > 0).astype(jnp.int32), (chip < chips - 1).astype(jnp.int32)
+    pl.semaphore_wait(barrier, 3 + inside * (2 - core) + outside * (1 + core))
+    to_left = remote(jedge.at[0, :, pl.ds(0, radii)], jhalo.at[1], jh_send.at[0], jh_recv.at[1], shell, left)
+    to_right = remote(jedge.at[1, :, pl.ds(0, radii)], jhalo.at[0], jh_send.at[1], jh_recv.at[0], shell, right)
+    to_left.start()
+    to_right.start()
+
+    def chain(step_at):
+        @pl.when(step_at)
+        def _():
+            @pl.when(chip < chips - 1)
+            def _():
+                pl.semaphore_wait(up_ready, 1)
+
+            @pl.when(chip > 0)
+            def _():
+                pl.semaphore_signal(up_ready, inc=1, device_id=(shell - 2, patch), device_id_type=mesh_id)
+
+            pl.semaphore_signal(side_ready, inc=1, device_id=(partner, patch), device_id_type=mesh_id)
+
+    chain(chip == chips - 1)
+
+    def down(there):
+        return remote(j_hbm.at[:, 0], jnext, rad_sem.at[0], rad_sem.at[1], there, patch)
+
+    @pl.when(shell > 0)
+    def _():
+        down(shell - 1).start()
+
+    def pack_side(k, c):
+        for f in range(2):
+            jside[0, f, pl.ds(k, 1), :] = jp[f, k, PAD + 1:PAD + 2, :]
+            jside[1, f, pl.ds(k, 1), :] = jp[f, k, PAD + cols - 2:PAD + cols - 1, :]
+        return c
+
+    lax.fori_loop(0, radii, pack_side, 0, unroll=8)
+
+    def beta_step(k, next_a, next_b, total):
+        pa = 0.5 * (jp[0, k, above] - jp[0, k, below])
+        pb = 0.5 * (jp[1, k, above] - jp[1, k, below])
+        source, ja, jb = beta_terms(theta, jp[0, k, inner], jp[1, k, inner], next_a, next_b, pa, pb)
+        barj[0, k], barj[1, k] = ja, jb
+        total = total + source
+        bp[k, inner] = total
+        bedge[0, 1, pl.ds(k, 1), :] = total[1:2]
+        bedge[1, 0, pl.ds(k, 1), :] = total[cols - 2:cols - 1]
+        return total
+
+    zero = jnp.zeros((cols, lanes), f32)
+    total = zero
+    slices = 4
+    for i in range(slices):
+        stop = (i + 1) * radii // slices if i < slices - 1 else radii - 1
+        total = lax.fori_loop(
+            i * radii // slices, stop,
+            lambda k, t: beta_step(k, jp[0, k + 1, inner], jp[1, k + 1, inner], t), total, unroll=2)
+        if i < slices - 1:
+            chain(chip == chips - 2 - i)
+    for c in range(chips - 1 - slices, -1, -1):
+        chain(chip == c)
+
+    @pl.when(shell == shells - 1)
+    def _():
+        for f in range(2):
+            jnext[f] = jp[f, radii - 1, inner]
+
+    @pl.when(shell < shells - 1)
+    def _():
+        down(shell).wait_recv()
+
+    sum_b[...] = beta_step(radii - 1, jnext[0], jnext[1], total)
+    for f in range(2):
+        jedge[0, f, radii:radii + 1] = jnext[f, 0:1]
+        jedge[1, f, radii:radii + 1] = jnext[f, cols - 1:cols]
+    to_left.wait_recv()
+    to_right.wait_recv()
+    edge_sources = []
+    for side, (over, under) in enumerate(((jside.at[0], jhalo.at[0]), (jhalo.at[1], jside.at[1]))):
+        pa, pb = (0.5 * (over[f] - under[f]) for f in range(2))
+        source, ja, jb = beta_terms(
+            theta, jedge[side, 0, 0:radii], jedge[side, 1, 0:radii],
+            jedge[side, 0, 1:radii + 1], jedge[side, 1, 1:radii + 1], pa, pb)
+        rows_w[side, 0], rows_w[side, 1] = ja, jb
+        edge_sources.append(source)
+        at = side * (cols - 1)
+        sum_b[at:at + 1] = jnp.sum(source, axis=0, keepdims=True)
 
     def pieces(stage, own, part, tot, slots, both):
         half = own.shape[0] // 2
@@ -231,7 +226,7 @@
             for e in range(2)] for d in range(1, chips)]
         return near, far
 
-    def begin(stage, own, part, tot, slots, both, rims=None, lines=None):
+    def begin(stage, own, part, tot, slots, both, during, rims=None, lines=None):
         mine, half, first, sends = pieces(stage, own, part, tot, slots, both)
         first.start()
         if rims is not None:
@@ -246,6 +241,7 @@
                 for copy in near:
                     copy.start()
 
+        during()
         first.wait_recv()
         tot[mine] = own[mine] + part[mine]
         if rims is not None:
@@ -347,28 +343,47 @@
                 remote(pre.at[mine], pre.at[mine], fwd_sem.at[stage, 0], fwd_sem.at[stage, 1],
                        partner, patch).wait_send()
 
-    pl.semaphore_wait(barrier, 3 * shells - 1)
+    pl.semaphore_wait(side_ready, 1)
     b_left = remote(bedge.at[0], bhalo.at[1], edge_send.at[0], edge_recv.at[1], shell, left)
     b_right = remote(bedge.at[1], bhalo.at[0], edge_send.at[1], edge_recv.at[0], shell, right)
-    b_left.start()
-    b_right.start()
+
+    def finish_edges():
+        row = lax.broadcasted_iota(jnp.int32, (radii, lanes), 0)
+        for side in range(2):
+            x, shift = edge_sources[side], 1
+            while shift < radii:
+                x = x + jnp.where(row >= shift, pltpu.roll(x, shift, 0), 0.0)
+                shift *= 2
+            bedge[side, side] = x
+        b_left.start()
+        b_right.start()
+
+        def place(k, c):
+            for side in range(2):
+                at = side * (cols - 1)
+                bp[k, PAD + at:PAD + at + 1, :] = bedge[side, side, pl.ds(k, 1), :]
+                for f in range(2):
+                    barj[f, k, at:at + 1, :] = rows_w[side, f, pl.ds(k, 1), :]
+            for f in range(2):
+                jp[f, k, before, :] = jhalo[0, f, pl.ds(k, 1), :]
+                jp[f, k, after, :] = jhalo[1, f, pl.ds(k, 1), :]
+            return c
+
+        lax.fori_loop(0, radii, place, 0, unroll=4)
+
     rims_b = (rim_b, rtot_b, rpart_b, rslot_b)
-    begin(0, sum_b, part_b, tot_b, slot_b, True, rims_b, ((0, 1), (cols - 2, cols - 1)))
-
-    zero = jnp.zeros((cols, lanes), f32)
+    begin(0, sum_b, part_b, tot_b, slot_b, True, finish_edges, rims_b, ((0, 1), (cols - 2, cols - 1)))
 
     def local_step(k, carry):
-        se, sa, sb, sja, sjb, sba, sbb = carry
-        bp[k, PAD + 8:PAD + cols - 8] = b_in[k]
-        beta = jnp.concatenate([bp[k, PAD:PAD + 8], b_in[k], bp[k, PAD + cols - 8:PAD + cols]], axis=0)
+        se, sa, sb, sja, sjb = carry
+        beta = bp[k, inner]
         grow = jnp.exp((2.0 * step) * beta)
         es[k, inner] = grow
         dr[k, inner] = theta(beta)
         a, b = jp[0, k, inner], jp[1, k, inner]
-        ja, jb = whole(barj_e, barj_in, 0, k), whole(barj_e, barj_in, 1, k)
-        return (se + grow, sa + a, sb + b, sja + ja, sjb + jb, sba + beta * a, sbb + beta * b)
-
-    se, sa, sb, sja, sjb, sba, sbb = lax.fori_loop(0, radii, local_step, (zero,) * 7, unroll=2)
+        return (se + grow, sa + a, sb + b, sja + barj[0, k], sjb + barj[1, k])
+
+    se, sa, sb, sja, sjb = lax.fori_loop(0, radii, local_step, (zero,) * 5, unroll=2)
     b_left.wait_recv()
     b_right.wait_recv()
 
@@ -416,9 +431,6 @@
     ua_sum, ub_sum = lax.fori_loop(0, radii, u_step, (wide_zero, wide_zero), unroll=2)
     sum_u[:cols] = ua_sum[1:cols + 1]
     sum_u[cols:] = ub_sum[1:cols + 1]
-    rims_u = (rim_u, rtot_u, rpart_u, rslot_u)
-    begin(1, sum_u, part_u, tot_u, slot_u, False, rims_u, ((0, cols), (cols - 1, 2 * cols - 1)))
-
     full_b = bt[inner]
     grow_b = jnp.exp((2.0 * step) * full_b)
 
@@ -431,7 +443,7 @@
         ta, tb = theta(ua), theta(ub)
         pa = 0.5 * (up[0, k, above] - up[0, k, below])
         pb = 0.5 * (up[1, k, above] - up[1, k, below])
-        ja, jb = whole(barj_e, barj_in, 0, k), whole(barj_e, barj_in, 1, k)
+        ja, jb = barj[0, k], barj[1, k]
         sw = sw + (growth * (ta + pb) + (b * ua - a * ub))
         ha = ha + ((ta - pb) + ua * ja - ub * jb + beta * a)
         hb = hb + ((tb + pa) + ua * jb + ub * ja + beta * b)
@@ -440,7 +452,13 @@
         ch[1, k] = hb
         return sw, ha, hb
 
-    sw, ha, hb = lax.fori_loop(0, radii, wh_step, (zero, zero, zero))
+    done = []
+    ahead = radii // 4
+    rims_u = (rim_u, rtot_u, rpart_u, rslot_u)
+    begin(1, sum_u, part_u, tot_u, slot_u, False,
+          lambda: done.extend(lax.fori_loop(0, ahead, wh_step, (zero, zero, zero))),
+          rims_u, ((0, cols), (cols - 1, 2 * cols - 1)))
+    sw, ha, hb = lax.fori_loop(ahead, radii, wh_step, tuple(done))
     end(1, sum_u, part_u, tot_u, slot_u, pre_u, below_u, False, rims_u)
     for f in range(2):
         ct[f] = jnp.zeros(ct.shape[1:], f32)
@@ -453,15 +471,21 @@
     sum_h[:cols] = sw + (grow_b * se) * re_bar + (sb * ca - sa * cb)
     sum_h[cols:2 * cols] = ha + n * eth_a + (ca * sja - cb * sjb)
     sum_h[2 * cols:] = hb + n * eth_b + (ca * sjb + cb * sja)
-    begin(2, sum_h, part_h, tot_h, slot_h, False)
 
     def fields_step(k, c):
         bfin[k] = step * (bp[k, inner] + full_b)
         gs[k] = grow_b * es[k, inner]
         return c
 
-    lax.fori_loop(0, radii, fields_step, 0, unroll=2)
+    begin(2, sum_h, part_h, tot_h, slot_h, False, lambda: lax.fori_loop(0, radii, fields_step, 0, unroll=2))
     end(2, sum_h, part_h, tot_h, slot_h, pre_h, below_h, False)
+    to_left.wait_send()
+    to_right.wait_send()
+
+    @pl.when(shell > 0)
+    def _():
+        down(shell - 1).wait_send()
+
     b_left.wait_send()
     b_right.wait_send()
     finish(0, sum_b, part_b, tot_b, slot_b, pre_b, True, rims_b)
@@ -469,7 +493,7 @@
     finish(2, sum_h, part_h, tot_h, slot_h, pre_h, False)
 
 
-def tail(step, jp, barj_in, barj_e, up, bfin, gs, cw, ch, ct, below_h, beta_out, u_out, w_out, h_out, uv, wv, hv, sems):
+def tail(step, jp, barj, up, bfin, gs, cw, ch, ct, below_h, beta_out, u_out, w_out, h_out, uv, wv, hv, sems):
     radii, cols, lanes = cw.shape
     inner = slice(PAD, PAD + cols)
     above = slice(PAD + 1, PAD + cols + 1)
@@ -484,7 +508,7 @@
     def final(k, carry):
         dw, da, db = carry
         a, b = jp[0, k, inner], jp[1, k, inner]
-        ja, jb = whole(barj_e, barj_in, 0, k), whole(barj_e, barj_in, 1, k)
+        ja, jb = barj[0, k], barj[1, k]
         dw = dw + (gs[k] * re_bar + (b * ca - a * cb))
         da = da + (eth_a + (ca * ja - cb * jb))
         db = db + (eth_b + (ca * jb + cb * ja))
@@ -526,46 +550,38 @@
         vmem = pl.BlockSpec(memory_space=pltpu.VMEM)
         hbm = pl.BlockSpec(memory_space=pltpu.HBM)
         plain, pair = (radii, cols, lanes), (2, radii, cols, lanes)
-        padded, middle = (2, radii, tall, lanes), (radii, cols - 16, lanes)
+        padded = (2, radii, tall, lanes)
         limit = 24 * 1024 * 1024
-        jp, jnext, b_in, barj_in = pl.pallas_call(
-            functools.partial(gather, shells, patches),
-            out_shape=(shape(*padded), shape(2, cols, lanes), shape(*middle), shape(2, *middle)),
-            in_specs=[hbm],
-            out_specs=(vmem,) * 4,
-            scratch_shapes=[vm(2, cols, lanes), vm(2, 2, radii, lanes), vm(2, 2, radii, lanes),
-                            dma, dma((2,)), dma((2,)), dma((2,))],
-            compiler_params=pltpu.CompilerParams(
-                collective_id=0, has_side_effects=True, vmem_limit_bytes=limit),
-        )(pltpu.with_memory_space_constraint(field_j, pltpu.HBM))
-
         many = max(chips - 1, 1)
-        scratch = [vm(radii, tall, lanes)] * 3 + [vm(tall, lanes), vm(2, 2, radii, lanes), vm(2, 2, radii, lanes),
-                                                  vm(cols, lanes), vm(2 * cols, lanes)]
+        regular = pltpu.SemaphoreType.REGULAR
+        planes = vm(2, 2, radii, lanes)
+        scratch = [vm(radii, tall, lanes)] * 3 + [vm(tall, lanes), planes, planes, vm(cols, lanes), vm(2 * cols, lanes),
+                                                  vm(2, cols, lanes), vm(2, 2, radii + 8, lanes), planes, planes, planes]
         for n in (1, 2, 3):
             scratch += [vm(n * cols, lanes)] * 3 + [vm(many, n * cols, lanes), vm(n * cols, lanes)]
         for _ in range(2):
             scratch += [vm(2, 2, lanes)] * 3 + [vm(many, 2, 2, lanes)]
-        scratch += [dma((2,)), dma((2,)), dma((3, 2)), dma((3, many, 2)), dma((3, many, 2)), dma((3, 2)),
+        scratch += [dma, dma((2,)), dma((2,)), dma((2,)), regular, regular,
+                    dma((2,)), dma((2,)), dma((3, 2)), dma((3, many, 2)), dma((3, many, 2)), dma((3, 2)),
                     dma((2, 2)), dma((2, 2)), dma((2, many, 2)), dma((2, many, 2))]
-        up, bfin, gs, cw, ch, ct, below_h, barj_e = pl.pallas_call(
+        found = pl.pallas_call(
             functools.partial(kernel, shells, patches, step),
-            out_shape=(shape(*padded), shape(*plain), shape(*plain), shape(*plain), shape(*pair),
-                       shape(2, tall, lanes), shape(3 * cols, lanes), shape(2, 2, radii, 8, lanes)),
-            in_specs=[vmem] * 4,
-            out_specs=(vmem,) * 8,
+            out_shape=(shape(*padded), shape(*pair), shape(*padded), shape(*plain), shape(*plain), shape(*plain),
+                       shape(*pair), shape(2, tall, lanes), shape(3 * cols, lanes)),
+            in_specs=[hbm],
+            out_specs=(vmem,) * 9,
             scratch_shapes=scratch,
             compiler_params=pltpu.CompilerParams(
-                collective_id=1, has_side_effects=True, vmem_limit_bytes=limit),
-        )(jp, jnext, b_in, barj_in)
+                collective_id=0, has_side_effects=True, vmem_limit_bytes=limit),
+        )(pltpu.with_memory_space_constraint(field_j, pltpu.HBM))
         return pl.pallas_call(
             functools.partial(tail, step),
             out_shape=(shape(*plain), shape(*pair), shape(*plain), shape(*pair)),
-            in_specs=[vmem] * 10,
+            in_specs=[vmem] * 9,
             out_specs=(hbm,) * 4,
             scratch_shapes=[vm(*pair), vm(*plain), vm(*pair), dma((4, 4))],
             compiler_params=pltpu.CompilerParams(vmem_limit_bytes=limit),
-        )(jp, barj_in, barj_e, up, bfin, gs, cw, ch, ct, below_h)
+        )(*found)
 
     return jax.shard_map(
         local,

time: 28.9 us -> 25.7 us (0.89)
  Pallas kernels: 28.1 us -> 24.9 us
    pallas_call x1 -> x0, Pallas kernels: 5.25 us -> none  [local(): pl.pallas_call(functools.partial(gather, shells, patches), out_shape=(sha...]
    pallas_call x1, Pallas kernels: 21 us -> 23.1 us  [local(): pl.pallas_call(functools.partial(kernel, shells, patches, step), out_shap...]
where the time goes in v3:
time: 25.7 us; the launch traced here: 25.5 us
  Pallas kernels  24.9 us (97%)
  between operations  0.64 us (2%)
    pallas_call x1, Pallas kernels, local(): pl.pallas_call(functools.partial(kernel, shells, patches, step), out_shap...  23.1 us
    pallas_call x1, Pallas kernels, local(): pl.pallas_call(functools.partial(tail, step), out_shape=(shape(*plain), s...  1.83 us

profile of v3, /device:TPU:25, one launch (start us, length us, event | category | flops | bytes accessed | tf_op | source)
XLA Modules:
  0.0 25.5 jit_solution(4824425769244756589)
XLA Ops:
  0.6 23.1 %shard_map.46 = (f32[2,32,48,128]{3,2,1,0:T(8,128)S(1)}, f32[2,32,32,128]{3,2,1,0:T(8,128)S(1)}, f32[2,32,48,128]{3,2,1,0:T(8,128)S(1)}, f32[32,32,128]{2,1,0:T(...) custom-call(f32[2,32,32,128]{3,2,1,0:T(8,128)} %j_hbm.1), custom_call_target="tpu_custom_call" | custom-call | tf_op jit(solution)/shard_map/pallas_call | solution.py:567
  23.7 1.8 %shard_map.47 = (f32[32,32,128]{2,1,0:T(8,128)}, f32[2,32,32,128]{3,2,1,0:T(8,128)}, f32[32,32,128]{2,1,0:T(8,128)}, f32[2,32,32,128]{3,2,1,0:T(8,128)}) custom-call(f32[2,32,48,128]{3,2,1,0:T(8,128)S(1)} %get-tuple-element.13.jp, f32[2,32,32,128]{3,2,1,0:T(8,128)S(1)} %get-tuple-element.14.barj, f32[2,32,48,128]{3,2,1,0:T(8,128)S(1)} %get-tuple-element.15.up, ...), custom_call_target="tpu_custom_call" | custom-call | tf_op jit(solution)/shard_map/pallas_call | solution.py:577

commit v4 on v3

--- a/solution.py
+++ b/solution.py
@@ -50,14 +50,14 @@
     return 0.25 * (0.5 * (ra * ra + rb * rb) - (ea * ea + eb * eb)), ta + pb, tb - pa
 
 
-def kernel(shells, patches, step, j_hbm, jp, barj, up, bfin, gs, cw, ch, ct, below_h,
-           bp, es, dr, bt, bedge, bhalo, below_b, below_u, jnext, jedge, jside, jhalo, rows_w,
-           sum_b, part_b, tot_b, slot_b, pre_b,
-           sum_u, part_u, tot_u, slot_u, pre_u,
-           sum_h, part_h, tot_h, slot_h, pre_h,
+def kernel(shells, patches, step, j_hbm, bfin, ufin, cw, ch, below_h,
+           jp, barj, up, ct, bp, es, dr, bt, bedge, bhalo, below_b, below_u, jnext, jedge, jside, jhalo, rows_w,
+           sum_b, part_b, tot_b, slot_b,
+           sum_u, part_u, tot_u, slot_u,
+           sum_h, part_h, tot_h, slot_h,
            rim_b, rtot_b, rpart_b, rslot_b, rim_u, rtot_u, rpart_u, rslot_u,
            load_sem, rad_sem, jh_send, jh_recv, up_ready, side_ready,
-           edge_send, edge_recv, part_sem, send_sem, recv_sem, fwd_sem,
+           edge_recv, part_send, part_recv, send_sem, recv_sem,
            rpart_send, rpart_recv, rim_send, rim_recv):
     radii, cols, lanes = cw.shape
     tall = cols + 8
@@ -167,10 +167,8 @@
         total = lax.fori_loop(
             i * radii // slices, stop,
             lambda k, t: beta_step(k, jp[0, k + 1, inner], jp[1, k + 1, inner], t), total, unroll=2)
-        if i < slices - 1:
-            chain(chip == chips - 2 - i)
-    for c in range(chips - 1 - slices, -1, -1):
-        chain(chip == c)
+        if i == slices // 2 - 1 and chips > 1:
+            chain(chip == chips - 2)
 
     @pl.when(shell == shells - 1)
     def _():
@@ -185,8 +183,12 @@
     for f in range(2):
         jedge[0, f, radii:radii + 1] = jnext[f, 0:1]
         jedge[1, f, radii:radii + 1] = jnext[f, cols - 1:cols]
+    for c in range(chips - 3, 0, -1):
+        chain(chip == c)
     to_left.wait_recv()
     to_right.wait_recv()
+    to_left.wait_send()
+    to_right.wait_send()
     edge_sources = []
     for side, (over, under) in enumerate(((jside.at[0], jhalo.at[0]), (jhalo.at[1], jside.at[1]))):
         pa, pb = (0.5 * (over[f] - under[f]) for f in range(2))
@@ -198,36 +200,29 @@
         at = side * (cols - 1)
         sum_b[at:at + 1] = jnp.sum(source, axis=0, keepdims=True)
 
-    def pieces(stage, own, part, tot, slots, both):
+    def pieces(stage, own, part, tot, slots):
         half = own.shape[0] // 2
         mine = pl.ds(pl.multiple_of(core * half, 8), half)
-        first = remote(own, part, part_sem.at[stage, 0], part_sem.at[stage, 1], partner, patch)
-        sends = []
-        for d in range(1, chips):
-            if both:
-                sends.append([
-                    remote(tot.at[mine], slots.at[d - 1, mine], send_sem.at[stage, d - 1, e],
-                           recv_sem.at[stage, d - 1, core], (chip + d) * 2 + e, patch)
-                    for e in range(2)])
-            else:
-                sends.append([
-                    remote(tot.at[mine], slots.at[d - 1, mine], send_sem.at[stage, d - 1, 0],
-                           recv_sem.at[stage, d - 1, 0], (chip + d) * 2 + core, patch)])
+        first = remote(own, part, part_send, part_recv.at[stage], partner, patch)
+        sends = [[
+            remote(tot.at[mine], slots.at[d - 1, mine], send_sem.at[d - 1, e],
+                   recv_sem.at[stage, d - 1, core], (chip + d) * 2 + e, patch)
+            for e in range(2)] for d in range(1, chips)]
         return mine, half, first, sends
 
     def rim_pieces(stage, rim, rtot, rpart, rslot):
         over = left * (1 - core) + right * core
         near = [
-            remote(rim.at[0], rpart.at[1], rpart_send.at[stage, 0], rpart_recv.at[stage, 1], partner, left),
-            remote(rim.at[1], rpart.at[0], rpart_send.at[stage, 1], rpart_recv.at[stage, 0], partner, right)]
+            remote(rim.at[0], rpart.at[1], rpart_send.at[0], rpart_recv.at[stage, 1], partner, left),
+            remote(rim.at[1], rpart.at[0], rpart_send.at[1], rpart_recv.at[stage, 0], partner, right)]
         far = [[
-            remote(rtot.at[core], rslot.at[d - 1, 1 - core], rim_send.at[stage, d - 1, e],
+            remote(rtot.at[core], rslot.at[d - 1, 1 - core], rim_send.at[d - 1, e],
                    rim_recv.at[stage, d - 1, 1 - core], (chip + d) * 2 + e, over)
             for e in range(2)] for d in range(1, chips)]
         return near, far
 
-    def begin(stage, own, part, tot, slots, both, during, rims=None, lines=None):
-        mine, half, first, sends = pieces(stage, own, part, tot, slots, both)
+    def begin(stage, own, part, tot, slots, during, rims=None, lines=None):
+        mine, half, first, sends = pieces(stage, own, part, tot, slots)
         first.start()
         if rims is not None:
             rim, rtot, rpart, rslot = rims
@@ -248,7 +243,7 @@
             for side in range(2):
                 for i, r in enumerate(lines[side]):
                     rtot[side, i:i + 1] = own[r:r + 1] + part[r:r + 1]
-        for d in range(1, chips):
+        for d in range(chips - 1, 0, -1):
             @pl.when(chip + d < chips)
             def _():
                 for copy in sends[d - 1]:
@@ -257,8 +252,8 @@
                     for copy in far[d - 1]:
                         copy.start()
 
-    def end(stage, own, part, tot, slots, pre, out, both, rims=None):
-        mine, half, first, sends = pieces(stage, own, part, tot, slots, both)
+    def end(stage, own, part, tot, slots, out, rims=None):
+        mine, half, first, sends = pieces(stage, own, part, tot, slots)
         if rims is not None:
             rim, rtot, rpart, rslot = rims
             near, far = rim_pieces(stage, rim, rtot, rpart, rslot)
@@ -279,46 +274,26 @@
             def _():
                 rpart[...] = jnp.zeros_like(rpart)
 
-        if both:
-            for d in range(1, chips):
-                @pl.when(chip >= d)
-                def _():
-                    for e in range(2):
-                        piece = pl.ds(e * half, half)
-                        remote(tot.at[piece], slots.at[d - 1, piece], send_sem.at[stage, d - 1, e],
-                               recv_sem.at[stage, d - 1, e], shell, patch).wait_recv()
-                    out[...] += slots[d - 1]
-        else:
-            @pl.when(chip > 0)
-            def _():
-                pre[mine] = jnp.zeros((half, lanes), f32)
-
-            for d in range(1, chips):
-                @pl.when(chip >= d)
-                def _():
-                    for copy in sends[d - 1]:
-                        copy.wait_recv()
-                    pre[mine] += slots[d - 1, mine]
-
-            @pl.when(chip > 0)
-            def _():
-                fwd = remote(pre.at[mine], pre.at[mine], fwd_sem.at[stage, 0], fwd_sem.at[stage, 1],
-                             partner, patch)
-                fwd.start()
-                fwd.wait_recv()
-                out[...] += pre[...]
+        for d in range(1, chips):
+            @pl.when(chip >= d)
+            def _():
+                for e in range(2):
+                    piece = pl.ds(e * half, half)
+                    remote(tot.at[piece], slots.at[d - 1, piece], send_sem.at[d - 1, e],
+                           recv_sem.at[stage, d - 1, e], shell, patch).wait_recv()
+                out[...] += slots[d - 1]
 
         if rims is not None:
             for d in range(1, chips):
                 @pl.when(chip >= d)
                 def _():
                     for e in range(2):
-                        remote(rtot.at[e], rslot.at[d - 1, e], rim_send.at[stage, d - 1, 0],
+                        remote(rtot.at[e], rslot.at[d - 1, e], rim_send.at[d - 1, 0],
                                rim_recv.at[stage, d - 1, e], shell, patch).wait_recv()
                     rpart[...] += rslot[d - 1]
 
-    def finish(stage, own, part, tot, slots, pre, both, rims=None):
-        mine, half, first, sends = pieces(stage, own, part, tot, slots, both)
+    def finish(stage, own, part, tot, slots, rims=None):
+        mine, half, first, sends = pieces(stage, own, part, tot, slots)
         first.wait_send()
         if rims is not None:
             near, far = rim_pieces(stage, *rims)
@@ -337,15 +312,11 @@
                     for copy in far[d - 1]:
                         copy.wait_send()
 
-        if not both:
-            @pl.when(chip > 0)
-            def _():
-                remote(pre.at[mine], pre.at[mine], fwd_sem.at[stage, 0], fwd_sem.at[stage, 1],
-                       partner, patch).wait_send()
-
+    if chips > 2:
+        chain(chip == 0)
     pl.semaphore_wait(side_ready, 1)
-    b_left = remote(bedge.at[0], bhalo.at[1], edge_send.at[0], edge_recv.at[1], shell, left)
-    b_right = remote(bedge.at[1], bhalo.at[0], edge_send.at[1], edge_recv.at[0], shell, right)
+    b_left = remote(bedge.at[0], bhalo.at[1], jh_send.at[0], edge_recv.at[1], shell, left)
+    b_right = remote(bedge.at[1], bhalo.at[0], jh_send.at[1], edge_recv.at[0], shell, right)
 
     def finish_edges():
         row = lax.broadcasted_iota(jnp.int32, (radii, lanes), 0)
@@ -372,7 +343,7 @@
         lax.fori_loop(0, radii, place, 0, unroll=4)
 
     rims_b = (rim_b, rtot_b, rpart_b, rslot_b)
-    begin(0, sum_b, part_b, tot_b, slot_b, True, finish_edges, rims_b, ((0, 1), (cols - 2, cols - 1)))
+    begin(0, sum_b, part_b, tot_b, slot_b, finish_edges, rims_b, ((0, 1), (cols - 2, cols - 1)))
 
     def local_step(k, carry):
         se, sa, sb, sja, sjb = carry
@@ -404,7 +375,8 @@
 
     lax.fori_loop(0, radii, halo_exp, 0, unroll=4)
     bt[...] = jnp.zeros_like(bt)
-    end(0, sum_b, part_b, tot_b, slot_b, pre_b, below_b, True, rims_b)
+    end(0, sum_b, part_b, tot_b, slot_b, below_b, rims_b)
+    finish(0, sum_b, part_b, tot_b, slot_b, rims_b)
     bt[inner] = below_b[...]
     bt[PAD - 2:PAD] = rpart_b[0]
     bt[PAD + cols:PAD + cols + 2] = rpart_b[1]
@@ -455,11 +427,12 @@
     done = []
     ahead = radii // 4
     rims_u = (rim_u, rtot_u, rpart_u, rslot_u)
-    begin(1, sum_u, part_u, tot_u, slot_u, False,
+    begin(1, sum_u, part_u, tot_u, slot_u,
           lambda: done.extend(lax.fori_loop(0, ahead, wh_step, (zero, zero, zero))),
           rims_u, ((0, cols), (cols - 1, 2 * cols - 1)))
     sw, ha, hb = lax.fori_loop(ahead, radii, wh_step, tuple(done))
-    end(1, sum_u, part_u, tot_u, slot_u, pre_u, below_u, False, rims_u)
+    end(1, sum_u, part_u, tot_u, slot_u, below_u, rims_u)
+    finish(1, sum_u, part_u, tot_u, slot_u, rims_u)
     for f in range(2):
         ct[f] = jnp.zeros(ct.shape[1:], f32)
         ct[f, inner] = below_u[f * cols:(f + 1) * cols]
@@ -472,15 +445,24 @@
     sum_h[cols:2 * cols] = ha + n * eth_a + (ca * sja - cb * sjb)
     sum_h[2 * cols:] = hb + n * eth_b + (ca * sjb + cb * sja)
 
-    def fields_step(k, c):
+    def fields_step(k, carry):
+        dw, da, db = carry
+        a, b = jp[0, k, inner], jp[1, k, inner]
+        ja, jb = barj[0, k], barj[1, k]
+        dw = dw + ((grow_b * es[k, inner]) * re_bar + (b * ca - a * cb))
+        da = da + (eth_a + (ca * ja - cb * jb))
+        db = db + (eth_b + (ca * jb + cb * ja))
         bfin[k] = step * (bp[k, inner] + full_b)
-        gs[k] = grow_b * es[k, inner]
-        return c
-
-    begin(2, sum_h, part_h, tot_h, slot_h, False, lambda: lax.fori_loop(0, radii, fields_step, 0, unroll=2))
-    end(2, sum_h, part_h, tot_h, slot_h, pre_h, below_h, False)
-    to_left.wait_send()
-    to_right.wait_send()
+        ufin[0, k] = step * (up[0, k, inner] + ca)
+        ufin[1, k] = step * (up[1, k, inner] + cb)
+        cw[k] = cw[k] + dw
+        ch[0, k] = ch[0, k] + da
+        ch[1, k] = ch[1, k] + db
+        return dw, da, db
+
+    begin(2, sum_h, part_h, tot_h, slot_h, lambda: None)
+    lax.fori_loop(0, radii, fields_step, (zero, zero, zero), unroll=2)
+    end(2, sum_h, part_h, tot_h, slot_h, below_h)
 
     @pl.when(shell > 0)
     def _():
@@ -488,46 +470,31 @@
 
     b_left.wait_send()
     b_right.wait_send()
-    finish(0, sum_b, part_b, tot_b, slot_b, pre_b, True, rims_b)
-    finish(1, sum_u, part_u, tot_u, slot_u, pre_u, False, rims_u)
-    finish(2, sum_h, part_h, tot_h, slot_h, pre_h, False)
-
-
-def tail(step, jp, barj, up, bfin, gs, cw, ch, ct, below_h, beta_out, u_out, w_out, h_out, uv, wv, hv, sems):
-    radii, cols, lanes = cw.shape
-    inner = slice(PAD, PAD + cols)
-    above = slice(PAD + 1, PAD + cols + 1)
-    below = slice(PAD - 1, PAD + cols - 1)
-    theta = make_theta(lanes)
-    copies = [pltpu.make_async_copy(bfin, beta_out, sems.at[0, 0])]
-    copies[0].start()
-    ca, cb = ct[0, inner], ct[1, inner]
-    re_bar, eth_a, eth_b = eth_planes(theta, ct, inner, above, below)
+    finish(2, sum_h, part_h, tot_h, slot_h)
+
+
+def tail(step, bfin, ufin, cw, ch, below_h, beta_out, u_out, w_out, h_out, wv, hv, first_sems, sems):
+    radii, cols, _ = cw.shape
+    copies = [pltpu.make_async_copy(bfin, beta_out, first_sems.at[0]),
+              pltpu.make_async_copy(ufin, u_out, first_sems.at[1])]
+    for copy in copies:
+        copy.start()
+    w, ha, hb = (below_h[i * cols:(i + 1) * cols] for i in range(3))
     sq = step * step
 
-    def final(k, carry):
-        dw, da, db = carry
-        a, b = jp[0, k, inner], jp[1, k, inner]
-        ja, jb = barj[0, k], barj[1, k]
-        dw = dw + (gs[k] * re_bar + (b * ca - a * cb))
-        da = da + (eth_a + (ca * ja - cb * jb))
-        db = db + (eth_b + (ca * jb + cb * ja))
-        uv[0, k] = step * (up[0, k, inner] + ca)
-        uv[1, k] = step * (up[1, k, inner] + cb)
-        wv[k] = sq * (cw[k] + dw)
-        hv[0, k] = sq * (ch[0, k] + da)
-        hv[1, k] = sq * (ch[1, k] + db)
-        return dw, da, db
-
-    carry = tuple(below_h[i * cols:(i + 1) * cols] for i in range(3))
-    chunks = sems.shape[1]
+    def final(k, c):
+        wv[k] = sq * (cw[k] + w)
+        hv[0, k] = sq * (ch[0, k] + ha)
+        hv[1, k] = sq * (ch[1, k] + hb)
+        return c
+
+    chunks = sems.shape[0]
     size = radii // chunks
     for i in range(chunks):
-        carry = lax.fori_loop(i * size, (i + 1) * size, final, carry, unroll=2)
+        lax.fori_loop(i * size, (i + 1) * size, final, 0, unroll=4)
         at = pl.ds(i * size, size)
-        more = [pltpu.make_async_copy(uv.at[:, at], u_out.at[:, at], sems.at[1, i]),
-                pltpu.make_async_copy(wv.at[at], w_out.at[at], sems.at[2, i]),
-                pltpu.make_async_copy(hv.at[:, at], h_out.at[:, at], sems.at[3, i])]
+        more = [pltpu.make_async_copy(wv.at[at], w_out.at[at], sems.at[i, 0]),
+                pltpu.make_async_copy(hv.at[:, at], h_out.at[:, at], sems.at[i, 1])]
         for copy in more:
             copy.start()
         copies += more
@@ -555,21 +522,21 @@
         many = max(chips - 1, 1)
         regular = pltpu.SemaphoreType.REGULAR
         planes = vm(2, 2, radii, lanes)
-        scratch = [vm(radii, tall, lanes)] * 3 + [vm(tall, lanes), planes, planes, vm(cols, lanes), vm(2 * cols, lanes),
+        scratch = [vm(*padded), vm(*pair), vm(*padded), vm(2, tall, lanes)]
+        scratch += [vm(radii, tall, lanes)] * 3 + [vm(tall, lanes), planes, planes, vm(cols, lanes), vm(2 * cols, lanes),
                                                   vm(2, cols, lanes), vm(2, 2, radii + 8, lanes), planes, planes, planes]
         for n in (1, 2, 3):
-            scratch += [vm(n * cols, lanes)] * 3 + [vm(many, n * cols, lanes), vm(n * cols, lanes)]
+            scratch += [vm(n * cols, lanes)] * 3 + [vm(many, n * cols, lanes)]
         for _ in range(2):
             scratch += [vm(2, 2, lanes)] * 3 + [vm(many, 2, 2, lanes)]
         scratch += [dma, dma((2,)), dma((2,)), dma((2,)), regular, regular,
-                    dma((2,)), dma((2,)), dma((3, 2)), dma((3, many, 2)), dma((3, many, 2)), dma((3, 2)),
-                    dma((2, 2)), dma((2, 2)), dma((2, many, 2)), dma((2, many, 2))]
+                    dma((2,)), dma, dma((3,)), dma((many, 2)), dma((3, many, 2)),
+                    dma((2,)), dma((2, 2)), dma((many, 2)), dma((2, many, 2))]
         found = pl.pallas_call(
             functools.partial(kernel, shells, patches, step),
-            out_shape=(shape(*padded), shape(*pair), shape(*padded), shape(*plain), shape(*plain), shape(*plain),
-                       shape(*pair), shape(2, tall, lanes), shape(3 * cols, lanes)),
+            out_shape=(shape(*plain), shape(*pair), shape(*plain), shape(*pair), shape(3 * cols, lanes)),
             in_specs=[hbm],
-            out_specs=(vmem,) * 9,
+            out_specs=(vmem,) * 5,
             scratch_shapes=scratch,
             compiler_params=pltpu.CompilerParams(
                 collective_id=0, has_side_effects=True, vmem_limit_bytes=limit),
@@ -577,9 +544,9 @@
         return pl.pallas_call(
             functools.partial(tail, step),
             out_shape=(shape(*plain), shape(*pair), shape(*plain), shape(*pair)),
-            in_specs=[vmem] * 9,
+            in_specs=[vmem] * 5,
             out_specs=(hbm,) * 4,
-            scratch_shapes=[vm(*pair), vm(*plain), vm(*pair), dma((4, 4))],
+            scratch_shapes=[vm(*plain), vm(*pair), dma((2,)), dma((2, 2))],
             compiler_params=pltpu.CompilerParams(vmem_limit_bytes=limit),
         )(*found)
 

time: 25.7 us -> 26.4 us (1.027)
  Pallas kernels: 24.9 us -> 25.5 us
    pallas_call x1, Pallas kernels: 23.1 us -> 23.8 us  [local(): pl.pallas_call(functools.partial(kernel, shells, patches, step), out_shap...]
where the time goes in v4:
time: 26.4 us; the launch traced here: 26.2 us
  Pallas kernels  25.5 us (97%)
  between operations  0.64 us (2%)
    pallas_call x1, Pallas kernels, local(): pl.pallas_call(functools.partial(kernel, shells, patches, step), out_shap...  23.8 us
    pallas_call x1, Pallas kernels, local(): pl.pallas_call(functools.partial(tail, step), out_shape=(shape(*plain), s...  1.71 us

profile of v4, /device:TPU:25, one launch (start us, length us, event | category | flops | bytes accessed | tf_op | source)
XLA Modules:
  0.0 26.2 jit_solution(4047357135489205050)
XLA Ops:
  0.6 23.8 %shard_map.46 = (f32[32,32,128]{2,1,0:T(8,128)S(1)}, f32[2,32,32,128]{3,2,1,0:T(8,128)S(1)}, f32[32,32,128]{2,1,0:T(8,128)S(1)}, f32[2,32,32,128]{3,2,1,0:T(8,128)S(1)}, f32[96,128]{1,0:T(8,128)S(1)}) custom-call(f32[2,32,32,128]{3,2,1,0:T(8,128)} %j_hbm.1), custom_call_target="tpu_custom_call" | custom-call | tf_op jit(solution)/shard_map/pallas_call | solution.py:535
  24.4 1.7 %shard_map.47 = (f32[32,32,128]{2,1,0:T(8,128)}, f32[2,32,32,128]{3,2,1,0:T(8,128)}, f32[32,32,128]{2,1,0:T(8,128)}, f32[2,32,32,128]{3,2,1,0:T(8,128)}) custom-call(f32[32,32,128]{2,1,0:T(8,128)S(1)} %get-tuple-element.9.bfin, f32[2,32,32,128]{3,2,1,0:T(8,128)S(1)} %get-tuple-element.10.ufin, f32[32,32,128]{2,1,0:T(8,128)S(1)} %get-tuple-element.11.cw, ...), custom_call_target="tpu_custom_call" | custom-call | tf_op jit(solution)/shard_map/pallas_call | solution.py:544

commit v5 on v4

--- a/solution.py
+++ b/solution.py
@@ -53,11 +53,11 @@
 def kernel(shells, patches, step, j_hbm, bfin, ufin, cw, ch, below_h,
            jp, barj, up, ct, bp, es, dr, bt, bedge, bhalo, below_b, below_u, jnext, jedge, jside, jhalo, rows_w,
            sum_b, part_b, tot_b, slot_b,
-           sum_u, part_u, tot_u, slot_u,
-           sum_h, part_h, tot_h, slot_h,
+           sum_u, part_u, tot_u, slot_u, pre_u,
+           sum_h, part_h, tot_h, slot_h, pre_h,
            rim_b, rtot_b, rpart_b, rslot_b, rim_u, rtot_u, rpart_u, rslot_u,
-           load_sem, rad_sem, jh_send, jh_recv, up_ready, side_ready,
-           edge_recv, part_send, part_recv, send_sem, recv_sem,
+           load_sem, rad_sem, jh_send, jh_recv, next_ready, up_ready, side_ready,
+           edge_recv, part_send, part_recv, send_sem, recv_sem, fwd_send, fwd_recv,
            rpart_send, rpart_recv, rim_send, rim_recv):
     radii, cols, lanes = cw.shape
     tall = cols + 8
@@ -90,6 +90,10 @@
     def _():
         greet(shell - 2, patch)
 
+        @pl.when(chip > 1)
+        def _():
+            greet(shell - 4, patch)
+
         @pl.when(core == 0)
         def _():
             greet(shell - 1, patch)
@@ -97,6 +101,10 @@
     @pl.when(chip < chips - 1)
     def _():
         greet(shell + 2, patch)
+
+        @pl.when(chip < chips - 2)
+        def _():
+            greet(shell + 4, patch)
 
         @pl.when(core == 1)
         def _():
@@ -112,22 +120,31 @@
 
     lax.fori_loop(0, radii, pack, 0, unroll=8)
     inside, outside = (chip > 0).astype(jnp.int32), (chip < chips - 1).astype(jnp.int32)
-    pl.semaphore_wait(barrier, 3 + inside * (2 - core) + outside * (1 + core))
+    further = (chip > 1).astype(jnp.int32) + (chip < chips - 2).astype(jnp.int32)
+    pl.semaphore_wait(barrier, 3 + inside * (2 - core) + outside * (1 + core) + further)
     to_left = remote(jedge.at[0, :, pl.ds(0, radii)], jhalo.at[1], jh_send.at[0], jh_recv.at[1], shell, left)
     to_right = remote(jedge.at[1, :, pl.ds(0, radii)], jhalo.at[0], jh_send.at[1], jh_recv.at[0], shell, right)
     to_left.start()
     to_right.start()
 
+    @pl.when(chip > 0)
+    def _():
+        pl.semaphore_signal(next_ready, inc=1, device_id=(shell - 2, patch), device_id_type=mesh_id)
+
     def chain(step_at):
         @pl.when(step_at)
         def _():
             @pl.when(chip < chips - 1)
             def _():
+                pl.semaphore_wait(next_ready, 1)
+
+            @pl.when(chip < chips - 2)
+            def _():
                 pl.semaphore_wait(up_ready, 1)
 
-            @pl.when(chip > 0)
-            def _():
-                pl.semaphore_signal(up_ready, inc=1, device_id=(shell - 2, patch), device_id_type=mesh_id)
+            @pl.when(chip > 1)
+            def _():
+                pl.semaphore_signal(up_ready, inc=1, device_id=(shell - 4, patch), device_id_type=mesh_id)
 
             pl.semaphore_signal(side_ready, inc=1, device_id=(partner, patch), device_id_type=mesh_id)
 
@@ -204,11 +221,21 @@
         half = own.shape[0] // 2
         mine = pl.ds(pl.multiple_of(core * half, 8), half)
         first = remote(own, part, part_send, part_recv.at[stage], partner, patch)
-        sends = [[
-            remote(tot.at[mine], slots.at[d - 1, mine], send_sem.at[d - 1, e],
-                   recv_sem.at[stage, d - 1, core], (chip + d) * 2 + e, patch)
-            for e in range(2)] for d in range(1, chips)]
+        sends = []
+        for d in range(1, chips):
+            if stage == 0:
+                sends.append([
+                    remote(tot.at[mine], slots.at[d - 1, mine], send_sem.at[d - 1, e],
+                           recv_sem.at[d - 1, core], (chip + d) * 2 + e, patch)
+                    for e in range(2)])
+            else:
+                sends.append([
+                    remote(tot.at[mine], slots.at[d - 1, mine], send_sem.at[d - 1, 0],
+                           recv_sem.at[d - 1, 1 + stage], (chip + d) * 2 + core, patch)])
         return mine, half, first, sends
+
+    def forward(stage, pre, mine):
+        return remote(pre.at[mine], pre.at[mine], fwd_send, fwd_recv.at[stage - 1], partner, patch)
 
     def rim_pieces(stage, rim, rtot, rpart, rslot):
         over = left * (1 - core) + right * core
@@ -252,7 +279,7 @@
                     for copy in far[d - 1]:
                         copy.start()
 
-    def end(stage, own, part, tot, slots, out, rims=None):
+    def end(stage, own, part, tot, slots, out, rims=None, pre=None):
         mine, half, first, sends = pieces(stage, own, part, tot, slots)
         if rims is not None:
             rim, rtot, rpart, rslot = rims
@@ -274,14 +301,33 @@
             def _():
                 rpart[...] = jnp.zeros_like(rpart)
 
-        for d in range(1, chips):
-            @pl.when(chip >= d)
-            def _():
-                for e in range(2):
-                    piece = pl.ds(e * half, half)
-                    remote(tot.at[piece], slots.at[d - 1, piece], send_sem.at[d - 1, e],
-                           recv_sem.at[stage, d - 1, e], shell, patch).wait_recv()
-                out[...] += slots[d - 1]
+        if stage == 0:
+            for d in range(1, chips):
+                @pl.when(chip >= d)
+                def _():
+                    for e in range(2):
+                        piece = pl.ds(e * half, half)
+                        remote(tot.at[piece], slots.at[d - 1, piece], send_sem.at[d - 1, e],
+                               recv_sem.at[d - 1, e], shell, patch).wait_recv()
+                    out[...] += slots[d - 1]
+        else:
+            @pl.when(chip > 0)
+            def _():
+                pre[mine] = jnp.zeros((half, lanes), f32)
+
+            for d in range(1, chips):
+                @pl.when(chip >= d)
+                def _():
+                    for copy in sends[d - 1]:
+                        copy.wait_recv()
+                    pre[mine] += slots[d - 1, mine]
+
+            @pl.when(chip > 0)
+            def _():
+                fwd = forward(stage, pre, mine)
+                fwd.start()
+                fwd.wait_recv()
+                out[...] += pre[...]
 
         if rims is not None:
             for d in range(1, chips):
@@ -292,7 +338,7 @@
                                rim_recv.at[stage, d - 1, e], shell, patch).wait_recv()
                     rpart[...] += rslot[d - 1]
 
-    def finish(stage, own, part, tot, slots, rims=None):
+    def finish(stage, own, part, tot, slots, rims=None, pre=None):
         mine, half, first, sends = pieces(stage, own, part, tot, slots)
         first.wait_send()
         if rims is not None:
@@ -311,6 +357,11 @@
                 if rims is not None:
                     for copy in far[d - 1]:
                         copy.wait_send()
+
+        if stage > 0:
+            @pl.when(chip > 0)
+            def _():
+                forward(stage, pre, mine).wait_send()
 
     if chips > 2:
         chain(chip == 0)
@@ -358,22 +409,21 @@
     b_left.wait_recv()
     b_right.wait_recv()
 
+    for side in range(2):
+        x = bhalo[side, 1 - side]
+        rows_w[side, 0] = jnp.exp((2.0 * step) * x)
+        rows_w[side, 1] = theta(x)
+
     def halo_step(k, c):
         for i in range(2):
             bp[k, PAD - 2 + i:PAD - 1 + i, :] = bhalo[0, i, pl.ds(k, 1), :]
             bp[k, PAD + cols + i:PAD + cols + i + 1, :] = bhalo[1, i, pl.ds(k, 1), :]
+        for side, at in enumerate((before, after)):
+            es[k, at, :] = rows_w[side, 0, pl.ds(k, 1), :]
+            dr[k, at, :] = rows_w[side, 1, pl.ds(k, 1), :]
         return c
 
-    lax.fori_loop(0, radii, halo_step, 0, unroll=8)
-
-    def halo_exp(k, c):
-        for lo in (0, PAD + cols):
-            x = bp[k, lo:lo + 8]
-            es[k, lo:lo + 8] = jnp.exp((2.0 * step) * x)
-            dr[k, lo:lo + 8] = theta(x)
-        return c
-
-    lax.fori_loop(0, radii, halo_exp, 0, unroll=4)
+    lax.fori_loop(0, radii, halo_step, 0, unroll=4)
     bt[...] = jnp.zeros_like(bt)
     end(0, sum_b, part_b, tot_b, slot_b, below_b, rims_b)
     finish(0, sum_b, part_b, tot_b, slot_b, rims_b)
@@ -431,8 +481,8 @@
           lambda: done.extend(lax.fori_loop(0, ahead, wh_step, (zero, zero, zero))),
           rims_u, ((0, cols), (cols - 1, 2 * cols - 1)))
     sw, ha, hb = lax.fori_loop(ahead, radii, wh_step, tuple(done))
-    end(1, sum_u, part_u, tot_u, slot_u, below_u, rims_u)
-    finish(1, sum_u, part_u, tot_u, slot_u, rims_u)
+    end(1, sum_u, part_u, tot_u, slot_u, below_u, rims_u, pre_u)
+    finish(1, sum_u, part_u, tot_u, slot_u, rims_u, pre_u)
     for f in range(2):
         ct[f] = jnp.zeros(ct.shape[1:], f32)
         ct[f, inner] = below_u[f * cols:(f + 1) * cols]
@@ -462,7 +512,7 @@
 
     begin(2, sum_h, part_h, tot_h, slot_h, lambda: None)
     lax.fori_loop(0, radii, fields_step, (zero, zero, zero), unroll=2)
-    end(2, sum_h, part_h, tot_h, slot_h, below_h)
+    end(2, sum_h, part_h, tot_h, slot_h, below_h, None, pre_h)
 
     @pl.when(shell > 0)
     def _():
@@ -470,7 +520,7 @@
 
     b_left.wait_send()
     b_right.wait_send()
-    finish(2, sum_h, part_h, tot_h, slot_h)
+    finish(2, sum_h, part_h, tot_h, slot_h, None, pre_h)
 
 
 def tail(step, bfin, ufin, cw, ch, below_h, beta_out, u_out, w_out, h_out, wv, hv, first_sems, sems):
@@ -526,11 +576,11 @@
         scratch += [vm(radii, tall, lanes)] * 3 + [vm(tall, lanes), planes, planes, vm(cols, lanes), vm(2 * cols, lanes),
                                                   vm(2, cols, lanes), vm(2, 2, radii + 8, lanes), planes, planes, planes]
         for n in (1, 2, 3):
-            scratch += [vm(n * cols, lanes)] * 3 + [vm(many, n * cols, lanes)]
+            scratch += [vm(n * cols, lanes)] * 3 + [vm(many, n * cols, lanes)] + [vm(n * cols, lanes)] * (n > 1)
         for _ in range(2):
             scratch += [vm(2, 2, lanes)] * 3 + [vm(many, 2, 2, lanes)]
-        scratch += [dma, dma((2,)), dma((2,)), dma((2,)), regular, regular,
-                    dma((2,)), dma, dma((3,)), dma((many, 2)), dma((3, many, 2)),
+        scratch += [dma, dma((2,)), dma((2,)), dma((2,)), regular, regular, regular,
+                    dma((2,)), dma, dma((3,)), dma((many, 2)), dma((many, 4)), dma, dma((2,)),
                     dma((2,)), dma((2, 2)), dma((many, 2)), dma((2, many, 2))]
         found = pl.pallas_call(
             functools.partial(kernel, shells, patches, step),

time: 26.4 us -> 24.8 us (0.939)
  Pallas kernels: 25.5 us -> 24 us
    pallas_call x1, Pallas kernels: 23.8 us -> 22.2 us  [local(): pl.pallas_call(functools.partial(kernel, shells, patches, step), out_shap...]
where the time goes in v5:
time: 24.8 us; the launch traced here: 24.6 us
  Pallas kernels  24 us (97%)
  between operations  0.64 us (3%)
    pallas_call x1, Pallas kernels, local(): pl.pallas_call(functools.partial(kernel, shells, patches, step), out_shap...  22.2 us
    pallas_call x1, Pallas kernels, local(): pl.pallas_call(functools.partial(tail, step), out_shape=(shape(*plain), s...  1.71 us

profile of v5, /device:TPU:25, one launch (start us, length us, event | category | flops | bytes accessed | tf_op | source)
XLA Modules:
  0.0 24.6 jit_solution(5988751479021992076)
XLA Ops:
  0.6 22.2 %shard_map.46 = (f32[32,32,128]{2,1,0:T(8,128)S(1)}, f32[2,32,32,128]{3,2,1,0:T(8,128)S(1)}, f32[32,32,128]{2,1,0:T(8,128)S(1)}, f32[2,32,32,128]{3,2,1,0:T(8,128)S(1)}, f32[96,128]{1,0:T(8,128)S(1)}) custom-call(f32[2,32,32,128]{3,2,1,0:T(8,128)} %j_hbm.1), custom_call_target="tpu_custom_call" | custom-call | tf_op jit(solution)/shard_map/pallas_call | solution.py:585
  22.9 1.7 %shard_map.47 = (f32[32,32,128]{2,1,0:T(8,128)}, f32[2,32,32,128]{3,2,1,0:T(8,128)}, f32[32,32,128]{2,1,0:T(8,128)}, f32[2,32,32,128]{3,2,1,0:T(8,128)}) custom-call(f32[32,32,128]{2,1,0:T(8,128)S(1)} %get-tuple-element.9.bfin, f32[2,32,32,128]{3,2,1,0:T(8,128)S(1)} %get-tuple-element.10.ufin, f32[32,32,128]{2,1,0:T(8,128)S(1)} %get-tuple-element.11.cw, ...), custom_call_target="tpu_custom_call" | custom-call | tf_op jit(solution)/shard_map/pallas_call | solution.py:594

commit v6 on v5

--- a/solution.py
+++ b/solution.py
@@ -86,18 +86,6 @@
     greet(shell, left)
     greet(shell, right)
 
-    @pl.when(chip > 0)
-    def _():
-        greet(shell - 2, patch)
-
-        @pl.when(chip > 1)
-        def _():
-            greet(shell - 4, patch)
-
-        @pl.when(core == 0)
-        def _():
-            greet(shell - 1, patch)
-
     @pl.when(chip < chips - 1)
     def _():
         greet(shell + 2, patch)
@@ -119,9 +107,8 @@
         return c
 
     lax.fori_loop(0, radii, pack, 0, unroll=8)
-    inside, outside = (chip > 0).astype(jnp.int32), (chip < chips - 1).astype(jnp.int32)
-    further = (chip > 1).astype(jnp.int32) + (chip < chips - 2).astype(jnp.int32)
-    pl.semaphore_wait(barrier, 3 + inside * (2 - core) + outside * (1 + core) + further)
+    inside, second = (chip > 0).astype(jnp.int32), (chip > 1).astype(jnp.int32)
+    pl.semaphore_wait(barrier, 3 + inside * (2 - core) + second)
     to_left = remote(jedge.at[0, :, pl.ds(0, radii)], jhalo.at[1], jh_send.at[0], jh_recv.at[1], shell, left)
     to_right = remote(jedge.at[1, :, pl.ds(0, radii)], jhalo.at[0], jh_send.at[1], jh_recv.at[0], shell, right)
     to_left.start()

time: 24.8 us -> 24.2 us (0.976)
  Pallas kernels: 24 us -> 23.3 us
    pallas_call x1, Pallas kernels: 22.2 us -> 21.6 us  [local(): pl.pallas_call(functools.partial(kernel, shells, patches, step), out_shap...]
where the time goes in v6:
time: 24.2 us; the launch traced here: 24 us
  Pallas kernels  23.3 us (96%)
  between operations  0.64 us (3%)
    pallas_call x1, Pallas kernels, local(): pl.pallas_call(functools.partial(kernel, shells, patches, step), out_shap...  21.6 us
    pallas_call x1, Pallas kernels, local(): pl.pallas_call(functools.partial(tail, step), out_shape=(shape(*plain), s...  1.71 us

profile of v6, /device:TPU:25, one launch (start us, length us, event | category | flops | bytes accessed | tf_op | source)
XLA Modules:
  0.0 24.0 jit_solution(4903475153607918374)
XLA Ops:
  0.6 21.6 %shard_map.46 = (f32[32,32,128]{2,1,0:T(8,128)S(1)}, f32[2,32,32,128]{3,2,1,0:T(8,128)S(1)}, f32[32,32,128]{2,1,0:T(8,128)S(1)}, f32[2,32,32,128]{3,2,1,0:T(8,128)S(1)}, f32[96,128]{1,0:T(8,128)S(1)}) custom-call(f32[2,32,32,128]{3,2,1,0:T(8,128)} %j_hbm.1), custom_call_target="tpu_custom_call" | custom-call | tf_op jit(solution)/shard_map/pallas_call | solution.py:572
  22.2 1.7 %shard_map.47 = (f32[32,32,128]{2,1,0:T(8,128)}, f32[2,32,32,128]{3,2,1,0:T(8,128)}, f32[32,32,128]{2,1,0:T(8,128)}, f32[2,32,32,128]{3,2,1,0:T(8,128)}) custom-call(f32[32,32,128]{2,1,0:T(8,128)S(1)} %get-tuple-element.9.bfin, f32[2,32,32,128]{3,2,1,0:T(8,128)S(1)} %get-tuple-element.10.ufin, f32[32,32,128]{2,1,0:T(8,128)S(1)} %get-tuple-element.11.cw, ...), custom_call_target="tpu_custom_call" | custom-call | tf_op jit(solution)/shard_map/pallas_call | solution.py:581

commit v7 on v6

--- a/solution.py
+++ b/solution.py
@@ -257,7 +257,7 @@
             for side in range(2):
                 for i, r in enumerate(lines[side]):
                     rtot[side, i:i + 1] = own[r:r + 1] + part[r:r + 1]
-        for d in range(chips - 1, 0, -1):
+        for d in (range(1, chips) if stage in (1,) else range(chips - 1, 0, -1)):
             @pl.when(chip + d < chips)
             def _():
                 for copy in sends[d - 1]:
@@ -350,23 +350,21 @@
             def _():
                 forward(stage, pre, mine).wait_send()
 
+    b_left = remote(bedge.at[0], bhalo.at[1], jh_send.at[0], edge_recv.at[1], shell, left)
+    b_right = remote(bedge.at[1], bhalo.at[0], jh_send.at[1], edge_recv.at[0], shell, right)
+    row = lax.broadcasted_iota(jnp.int32, (radii, lanes), 0)
+    for side in range(2):
+        x, shift = edge_sources[side], 1
+        while shift < radii:
+            x = x + jnp.where(row >= shift, pltpu.roll(x, shift, 0), 0.0)
+            shift *= 2
+        bedge[side, side] = x
+    b_left.start()
+    b_right.start()
     if chips > 2:
         chain(chip == 0)
     pl.semaphore_wait(side_ready, 1)
-    b_left = remote(bedge.at[0], bhalo.at[1], jh_send.at[0], edge_recv.at[1], shell, left)
-    b_right = remote(bedge.at[1], bhalo.at[0], jh_send.at[1], edge_recv.at[0], shell, right)
-
     def finish_edges():
-        row = lax.broadcasted_iota(jnp.int32, (radii, lanes), 0)
-        for side in range(2):
-            x, shift = edge_sources[side], 1
-            while shift < radii:
-                x = x + jnp.where(row >= shift, pltpu.roll(x, shift, 0), 0.0)
-                shift *= 2
-            bedge[side, side] = x
-        b_left.start()
-        b_right.start()
-
         def place(k, c):
             for side in range(2):
                 at = side * (cols - 1)

time: 24.2 us -> 23.6 us (0.975)
  Pallas kernels: 23.3 us -> 22.7 us
    pallas_call x1, Pallas kernels: 21.6 us -> 21 us  [local(): pl.pallas_call(functools.partial(kernel, shells, patches, step), out_shap...]
where the time goes in v7:
time: 23.6 us; the launch traced here: 23.3 us
  Pallas kernels  22.7 us (96%)
  between operations  0.64 us (3%)
    pallas_call x1, Pallas kernels, local(): pl.pallas_call(functools.partial(kernel, shells, patches, step), out_shap...  21 us
    pallas_call x1, Pallas kernels, local(): pl.pallas_call(functools.partial(tail, step), out_shape=(shape(*plain), s...  1.71 us

profile of v7, /device:TPU:25, one launch (start us, length us, event | category | flops | bytes accessed | tf_op | source)
XLA Modules:
  0.0 23.3 jit_solution(4614898607546808612)
XLA Ops:
  0.6 21.0 %shard_map.46 = (f32[32,32,128]{2,1,0:T(8,128)S(1)}, f32[2,32,32,128]{3,2,1,0:T(8,128)S(1)}, f32[32,32,128]{2,1,0:T(8,128)S(1)}, f32[2,32,32,128]{3,2,1,0:T(8,128)S(1)}, f32[96,128]{1,0:T(8,128)S(1)}) custom-call(f32[2,32,32,128]{3,2,1,0:T(8,128)} %j_hbm.1), custom_call_target="tpu_custom_call" | custom-call | tf_op jit(solution)/shard_map/pallas_call | solution.py:570
  21.6 1.7 %shard_map.47 = (f32[32,32,128]{2,1,0:T(8,128)}, f32[2,32,32,128]{3,2,1,0:T(8,128)}, f32[32,32,128]{2,1,0:T(8,128)}, f32[2,32,32,128]{3,2,1,0:T(8,128)}) custom-call(f32[32,32,128]{2,1,0:T(8,128)S(1)} %get-tuple-element.9.bfin, f32[2,32,32,128]{3,2,1,0:T(8,128)S(1)} %get-tuple-element.10.ufin, f32[32,32,128]{2,1,0:T(8,128)S(1)} %get-tuple-element.11.cw, ...), custom_call_target="tpu_custom_call" | custom-call | tf_op jit(solution)/shard_map/pallas_call | solution.py:579
